TPU v7x, 32 devices: a whole 2x2x4 slice. The times are simulated.
32 devices in a mesh: fsdp: 4 (over y, core), ctx: 8 (over z, x).
Axes of the slice: x: 2, y: 2, z: 4, core: 2. Of those that a mesh axis runs over, the one named last changes fastest.
Arguments:
- inputs: bfloat16 [4, 1024, 768], P('fsdp', 'ctx'), may hold values from -6 to 6
- lengths: int32 [4], P('fsdp'), may hold values from 512 to 1024, as said below
- ln1_gain: bfloat16 [768], P('fsdp'), may hold values from 0.25 to 1.75
- ln1_bias: bfloat16 [768], P('fsdp'), may hold values from -1.75 to 1.75
- qkv_weight: bfloat16 [768, 2304], P('fsdp'), may hold values from -0.3125 to 0.3125
- qv_bias: bfloat16 [1536], P('fsdp'), may hold values from -1.75 to 1.75
- out_weight: bfloat16 [768, 768], P('fsdp'), may hold values from -0.625 to 0.625
- out_bias: bfloat16 [768], P('fsdp'), may hold values from -1.75 to 1.75
- ln2_gain: bfloat16 [768], P('fsdp'), may hold values from 0.25 to 1.75
- ln2_bias: bfloat16 [768], P('fsdp'), may hold values from -1.75 to 1.75
- fc_weight: bfloat16 [768, 3072], P('fsdp'), may hold values from -0.21875 to 0.21875
- fc_bias: bfloat16 [3072], P('fsdp'), may hold values from -1.75 to 1.75
- proj_weight: bfloat16 [3072, 768], P('fsdp'), may hold values from -0.109375 to 0.109375
- proj_bias: bfloat16 [768], P('fsdp'), may hold values from -1.75 to 1.75
- cotangent: bfloat16 [4, 1024, 768], P('fsdp', 'ctx'), may hold values from -6 to 6
Outputs:
- outputs: bfloat16 [4, 1024, 768], P('fsdp', 'ctx')
- input_grad: bfloat16 [4, 1024, 768], P('fsdp', 'ctx')
- grad_ln1_gain: float32 [768], P('fsdp')
- grad_ln1_bias: float32 [768], P('fsdp')
- grad_qkv_weight: float32 [768, 2304], P('fsdp')
- grad_qv_bias: float32 [1536], P('fsdp')
- grad_out_weight: float32 [768, 768], P('fsdp')
- grad_out_bias: float32 [768], P('fsdp')
- grad_ln2_gain: float32 [768], P('fsdp')
- grad_ln2_bias: float32 [768], P('fsdp')
- grad_fc_weight: float32 [768, 3072], P('fsdp')
- grad_fc_bias: float32 [3072], P('fsdp')
- grad_proj_weight: float32 [3072, 768], P('fsdp')
- grad_proj_bias: float32 [768], P('fsdp')
Inputs may be any that keep to these rules, and one draw needn't show every extreme that they name: Sequence s holds tokens at its first lengths[s] positions and padding after them; in every draw some sequence fills its whole slot of 1024.
All inputs are finite; a program needn't handle non-finite values.
Results may differ from a plain program's by a relative error of at most 0.02.
Values may be sent and summed in bfloat16 or wider, within the bound.
No kernel may reach another device: no remote copies, remote signals or barrier semaphores. Data moves between devices by JAX's collectives and lax.ppermute only.
A program may use at most 128 MiB of HBM per device.

v0:
```python
import jax
import jax.numpy as jnp
from jax import lax
from jax.sharding import PartitionSpec as P

HD = 64


EPSILON = 1e-05
NEGATIVE = -1e30
FAR_ABOVE = 1e30
GELU_COEF = 0.7978845608028654


def from_behind(x, axis, by):
    count = lax.axis_size(axis)
    return lax.ppermute(x, axis, [(i, (i + by) % count) for i in range(count)])


def gelu_tanh(values):
    return (
        0.5 * values * (1.0 + jnp.tanh(GELU_COEF * (values + 0.044715 * values * values * values)))
    )


def norm_forward(values, ln_gain, ln_shift):
    centred = values - jnp.mean(values, axis=-1, keepdims=True)
    inverse = lax.rsqrt(jnp.mean(centred * centred, axis=-1, keepdims=True) + EPSILON)
    scaled = centred * inverse
    return (scaled * ln_gain + ln_shift, scaled, inverse)


def norm_backward(upstream, scaled, inverse, ln_gain):
    weighted = upstream * ln_gain
    inner_term = (
        weighted
        - jnp.mean(weighted, axis=-1, keepdims=True)
        - scaled * jnp.mean(weighted * scaled, axis=-1, keepdims=True)
    )
    return (inverse * inner_term, jnp.sum(upstream * scaled, axis=0), jnp.sum(upstream, axis=0))


def token_places(first_row, wanted_rows, shard_len):
    row_ids = first_row + lax.iota(jnp.int32, wanted_rows)
    owner_index = row_ids // shard_len
    inside = row_ids % shard_len
    return owner_index * shard_len + inside


def permitted(query_places, key_places, lengths):
    causal = key_places[None, :] <= query_places[:, None]
    inside = key_places[None, :] < lengths[:, None]
    return causal[None] & inside[:, None, :]


def over_blocks(piece_rows, shard_len, block_step, fold_state):
    if piece_rows <= 1024:
        block_rows = piece_rows
    elif piece_rows % 1024 == 0:
        block_rows = 1024
    else:
        block_rows = shard_len

    def run_block(turn_index, current):
        return block_step(current, turn_index * block_rows, block_rows)

    return lax.fori_loop(0, piece_rows // block_rows, run_block, fold_state)


def body(
    inputs,
    lengths,
    ln1_gain,
    ln1_bias,
    qkv_weight,
    qv_bias,
    out_weight,
    out_bias,
    ln2_gain,
    ln2_bias,
    fc_weight,
    fc_bias,
    proj_weight,
    proj_bias,
    cotangent,
):
    f32 = jnp.float32
    bf16 = jnp.bfloat16
    group_size = lax.axis_size("ctx")
    group_place = lax.axis_index("ctx")
    seq_count, shard_len, model_width = inputs.shape
    head_count = model_width // HD
    fetched = (
        lax.all_gather(ln1_gain, "fsdp", axis=0, tiled=True),
        lax.all_gather(ln1_bias, "fsdp", axis=0, tiled=True),
        lax.all_gather(qkv_weight, "fsdp", axis=0, tiled=True),
        lax.all_gather(qv_bias, "fsdp", axis=0, tiled=True),
        lax.all_gather(out_weight, "fsdp", axis=0, tiled=True),
        lax.all_gather(out_bias, "fsdp", axis=0, tiled=True),
        lax.all_gather(ln2_gain, "fsdp", axis=0, tiled=True),
        lax.all_gather(ln2_bias, "fsdp", axis=0, tiled=True),
        lax.all_gather(fc_weight, "fsdp", axis=0, tiled=True),
        lax.all_gather(fc_bias, "fsdp", axis=0, tiled=True),
        lax.all_gather(proj_weight, "fsdp", axis=0, tiled=True),
        lax.all_gather(proj_bias, "fsdp", axis=0, tiled=True),
    )
    (
        gain_one,
        shift_one,
        qkv_full,
        qv_full,
        out_full,
        out_shift,
        gain_two,
        shift_two,
        fc_full,
        fc_shift,
        proj_full,
        proj_shift,
    ) = fetched
    row_count = seq_count * shard_len
    flat_tokens = inputs.reshape(row_count, model_width).astype(f32)
    normed, scaled_one, inverse_one = norm_forward(
        flat_tokens, gain_one.astype(f32), shift_one.astype(f32)
    )
    normed_low = normed.astype(bf16)
    zero_bias = jnp.zeros((model_width,), f32)
    full_bias = jnp.concatenate(
        [qv_full[:model_width].astype(f32), zero_bias, qv_full[model_width:].astype(f32)]
    )
    projected = (jnp.dot(normed_low, qkv_full, preferred_element_type=f32) + full_bias).astype(bf16)
    queries = projected[:, :model_width].reshape(seq_count, shard_len, model_width)
    keys_own = projected[:, model_width : 2 * model_width].reshape(
        seq_count, shard_len, model_width
    )
    values_own = projected[:, 2 * model_width :].reshape(seq_count, shard_len, model_width)
    queries_split = queries.reshape(seq_count, shard_len, head_count, HD)
    query_places = token_places(group_place * shard_len, shard_len, shard_len)
    query_valid = query_places[None, :] < lengths[:, None]
    start_state = (
        jnp.full((seq_count, head_count, shard_len), NEGATIVE, f32),
        jnp.zeros((seq_count, head_count, shard_len), f32),
        jnp.zeros((seq_count, shard_len, head_count, HD), f32),
    )
    arrived_piece = (
        lax.all_gather(keys_own, "ctx", axis=1, tiled=True),
        lax.all_gather(values_own, "ctx", axis=1, tiled=True),
    )

    def block_step(current, offset, block_rows):
        key_block = lax.dynamic_slice_in_dim(arrived_piece[0], offset, block_rows, 1).reshape(
            seq_count, block_rows, head_count, HD
        )
        value_block = lax.dynamic_slice_in_dim(arrived_piece[1], offset, block_rows, 1).reshape(
            seq_count, block_rows, head_count, HD
        )
        key_places = token_places(offset, block_rows, shard_len)
        allowed = permitted(query_places, key_places, lengths)

        def block_compute(inner_state):
            row_top, row_total, row_acc = inner_state
            scores = (
                jnp.einsum("sqhd,skhd->shqk", queries_split, key_block, preferred_element_type=f32)
                * 0.125
            )
            scores = jnp.where(allowed[:, None], scores, NEGATIVE)
            new_top = jnp.maximum(row_top, jnp.max(scores, axis=-1))
            weights = jnp.where(allowed[:, None], jnp.exp(scores - new_top[..., None]), 0.0)
            rescale = jnp.exp(row_top - new_top)
            new_total = row_total * rescale + jnp.sum(weights, axis=-1)
            gathered = jnp.einsum(
                "shqk,skhd->sqhd", weights.astype(bf16), value_block, preferred_element_type=f32
            )
            new_acc = row_acc * jnp.transpose(rescale, (0, 2, 1))[..., None] + gathered
            return (new_top, new_total, new_acc)

        any_live = jnp.any(allowed & query_valid[:, :, None])
        return lax.cond(any_live, block_compute, lambda untouched: untouched, current)

    row_top, row_total, row_acc = over_blocks(
        arrived_piece[0].shape[1], shard_len, block_step, start_state
    )
    safe_total = jnp.where(row_total > 0.0, row_total, 1.0)
    attended = jnp.where(
        query_valid[:, :, None, None],
        row_acc / jnp.transpose(safe_total, (0, 2, 1))[..., None],
        0.0,
    )
    log_total = jnp.where(query_valid[:, None, :], row_top + jnp.log(safe_total), FAR_ABOVE)
    attended_low = attended.reshape(row_count, model_width).astype(bf16)
    branch = jnp.dot(attended_low, out_full, preferred_element_type=f32) + out_shift.astype(f32)
    residual = flat_tokens + branch
    normed_two, scaled_two, inverse_two = norm_forward(
        residual, gain_two.astype(f32), shift_two.astype(f32)
    )
    normed_two_low = normed_two.astype(bf16)
    hidden = jnp.dot(normed_two_low, fc_full, preferred_element_type=f32) + fc_shift.astype(f32)
    active_low = gelu_tanh(hidden).astype(bf16)
    result = jnp.dot(active_low, proj_full, preferred_element_type=f32) + proj_shift.astype(f32)
    row_valid = query_valid.reshape(row_count)[:, None]
    outputs = (
        jnp.where(row_valid, residual + result, 0.0)
        .astype(bf16)
        .reshape(seq_count, shard_len, model_width)
    )
    grad_output = jnp.where(row_valid, cotangent.reshape(row_count, model_width).astype(f32), 0.0)
    grad_result_low = grad_output.astype(bf16)
    grad_proj_shift = jnp.sum(grad_output, axis=0)
    grad_proj = jnp.dot(active_low.T, grad_result_low, preferred_element_type=f32)
    grad_active = jnp.dot(grad_result_low, proj_full.T, preferred_element_type=f32)
    gelu_pull = jax.vjp(gelu_tanh, hidden)[1]
    grad_hidden_low = gelu_pull(grad_active)[0].astype(bf16)
    grad_fc_shift = jnp.sum(grad_hidden_low, axis=0, dtype=f32)
    grad_fc = jnp.dot(normed_two_low.T, grad_hidden_low, preferred_element_type=f32)
    grad_normed_two = jnp.dot(grad_hidden_low, fc_full.T, preferred_element_type=f32)
    grad_through_two, grad_gain_two, grad_shift_two = norm_backward(
        grad_normed_two, scaled_two, inverse_two, gain_two.astype(f32)
    )
    grad_residual = grad_output + grad_through_two
    grad_branch_low = grad_residual.astype(bf16)
    grad_out_shift = jnp.sum(grad_branch_low, axis=0, dtype=f32)
    grad_out = jnp.dot(attended_low.T, grad_branch_low, preferred_element_type=f32)
    grad_attended_low = (
        jnp.dot(grad_branch_low, out_full.T, preferred_element_type=f32)
        .astype(bf16)
        .reshape(seq_count, shard_len, model_width)
    )
    grad_split = grad_attended_low.reshape(seq_count, shard_len, head_count, HD)
    delta_rows = jnp.transpose(jnp.sum(grad_split.astype(f32) * attended, axis=-1), (0, 2, 1))
    zero_grads = jnp.zeros((seq_count, shard_len, head_count, HD), f32)

    def cycle_turn(turn_index, cycle_state):
        grad_q_acc, moving_keys, moving_values, moving_gk, moving_gv = cycle_state
        anchor = (group_place + turn_index) % group_size
        key_places = token_places(anchor * shard_len, shard_len, shard_len)
        allowed = permitted(query_places, key_places, lengths)
        key_block = moving_keys.reshape(seq_count, shard_len, head_count, HD)
        value_block = moving_values.reshape(seq_count, shard_len, head_count, HD)

        def cycle_compute(inner_state):
            grad_q_now, grad_k_now, grad_v_now = inner_state
            scores = (
                jnp.einsum("sqhd,skhd->shqk", queries_split, key_block, preferred_element_type=f32)
                * 0.125
            )
            attention = jnp.where(allowed[:, None], jnp.exp(scores - log_total[..., None]), 0.0)
            grad_v_now = grad_v_now + jnp.einsum(
                "shqk,sqhd->skhd", attention.astype(bf16), grad_split, preferred_element_type=f32
            )
            grad_attention = jnp.einsum(
                "sqhd,skhd->shqk", grad_split, value_block, preferred_element_type=f32
            )
            grad_scores = (attention * (grad_attention - delta_rows[..., None])).astype(bf16)
            grad_q_now = (
                grad_q_now
                + jnp.einsum("shqk,skhd->sqhd", grad_scores, key_block, preferred_element_type=f32)
                * 0.125
            )
            grad_k_now = (
                grad_k_now
                + jnp.einsum(
                    "shqk,sqhd->skhd", grad_scores, queries_split, preferred_element_type=f32
                )
                * 0.125
            )
            return (grad_q_now, grad_k_now, grad_v_now)

        any_live = jnp.any(allowed & query_valid[:, :, None])
        grad_q_acc, moving_gk, moving_gv = lax.cond(
            any_live, cycle_compute, lambda untouched: untouched, (grad_q_acc, moving_gk, moving_gv)
        )
        moving_keys, moving_values = from_behind((moving_keys, moving_values), "ctx", -1)
        moving_gk, moving_gv = (
            from_behind(moving_gk.astype(jnp.bfloat16), "ctx", -1).astype(moving_gk.dtype),
            from_behind(moving_gv.astype(jnp.bfloat16), "ctx", -1).astype(moving_gv.dtype),
        )
        return (grad_q_acc, moving_keys, moving_values, moving_gk, moving_gv)

    cycle_final = lax.fori_loop(
        0, group_size, cycle_turn, (zero_grads, keys_own, values_own, zero_grads, zero_grads)
    )
    grad_queries = cycle_final[0]
    grad_keys = cycle_final[3]
    grad_values = cycle_final[4]
    grad_projected = jnp.concatenate(
        [
            grad_queries.reshape(row_count, model_width),
            grad_keys.reshape(row_count, model_width),
            grad_values.reshape(row_count, model_width),
        ],
        axis=1,
    ).astype(bf16)
    grad_qv = jnp.concatenate(
        [
            jnp.sum(grad_projected[:, :model_width], axis=0, dtype=f32),
            jnp.sum(grad_projected[:, 2 * model_width :], axis=0, dtype=f32),
        ]
    )
    grad_qkv = jnp.dot(normed_low.T, grad_projected, preferred_element_type=f32)
    grad_normed_one = jnp.dot(grad_projected, qkv_full.T, preferred_element_type=f32)
    grad_through_one, grad_gain_one, grad_shift_one = norm_backward(
        grad_normed_one, scaled_one, inverse_one, gain_one.astype(f32)
    )
    input_grad = (
        (grad_residual + grad_through_one).astype(bf16).reshape(seq_count, shard_len, model_width)
    )
    owned_all = (
        lax.psum_scatter(
            grad_gain_one.astype(jnp.bfloat16), "fsdp", scatter_dimension=0, tiled=True
        ).astype(jnp.float32),
        lax.psum_scatter(
            grad_shift_one.astype(jnp.bfloat16), "fsdp", scatter_dimension=0, tiled=True
        ).astype(jnp.float32),
        lax.psum_scatter(
            grad_qkv.astype(jnp.bfloat16), "fsdp", scatter_dimension=0, tiled=True
        ).astype(jnp.float32),
        lax.psum_scatter(
            grad_qv.astype(jnp.bfloat16), "fsdp", scatter_dimension=0, tiled=True
        ).astype(jnp.float32),
        lax.psum_scatter(
            grad_out.astype(jnp.bfloat16), "fsdp", scatter_dimension=0, tiled=True
        ).astype(jnp.float32),
        lax.psum_scatter(
            grad_out_shift.astype(jnp.bfloat16), "fsdp", scatter_dimension=0, tiled=True
        ).astype(jnp.float32),
        lax.psum_scatter(
            grad_gain_two.astype(jnp.bfloat16), "fsdp", scatter_dimension=0, tiled=True
        ).astype(jnp.float32),
        lax.psum_scatter(
            grad_shift_two.astype(jnp.bfloat16), "fsdp", scatter_dimension=0, tiled=True
        ).astype(jnp.float32),
        lax.psum_scatter(
            grad_fc.astype(jnp.bfloat16), "fsdp", scatter_dimension=0, tiled=True
        ).astype(jnp.float32),
        lax.psum_scatter(
            grad_fc_shift.astype(jnp.bfloat16), "fsdp", scatter_dimension=0, tiled=True
        ).astype(jnp.float32),
        lax.psum_scatter(
            grad_proj.astype(jnp.bfloat16), "fsdp", scatter_dimension=0, tiled=True
        ).astype(jnp.float32),
        lax.psum_scatter(
            grad_proj_shift.astype(jnp.bfloat16), "fsdp", scatter_dimension=0, tiled=True
        ).astype(jnp.float32),
    )
    summed = lax.psum(
        (
            owned_all[0],
            owned_all[1],
            owned_all[2],
            owned_all[3],
            owned_all[4],
            owned_all[5],
            owned_all[6],
            owned_all[7],
            owned_all[8],
            owned_all[9],
            owned_all[10],
            owned_all[11],
        ),
        "ctx",
    )
    return (
        outputs,
        input_grad,
        summed[0],
        summed[1],
        summed[2],
        summed[3],
        summed[4],
        summed[5],
        summed[6],
        summed[7],
        summed[8],
        summed[9],
        summed[10],
        summed[11],
    )


def solution(mesh):
    in_specs = (
        P("fsdp", "ctx", None),
        P("fsdp"),
        P("fsdp"),
        P("fsdp"),
        P("fsdp", None),
        P("fsdp"),
        P("fsdp", None),
        P("fsdp"),
        P("fsdp"),
        P("fsdp"),
        P("fsdp", None),
        P("fsdp"),
        P("fsdp", None),
        P("fsdp"),
        P("fsdp", "ctx", None),
    )
    out_specs = (
        P("fsdp", "ctx", None),
        P("fsdp", "ctx", None),
        P("fsdp"),
        P("fsdp"),
        P("fsdp", None),
        P("fsdp"),
        P("fsdp", None),
        P("fsdp"),
        P("fsdp"),
        P("fsdp"),
        P("fsdp", None),
        P("fsdp"),
        P("fsdp", None),
        P("fsdp"),
    )
    return jax.shard_map(body, mesh=mesh, in_specs=in_specs, out_specs=out_specs, check_vma=False)
```

profile of v0, /device:TPU:0, one launch (start us, length us, event | category | flops | bytes accessed | tf_op | source)
XLA Modules:
  0.0 880.3 jit_solution(389110238020825437)
XLA Ops:
  8.7 6.2 all-gather.2
  21.1 13.5 %all-reduce.16 = (bf16[768]{0:T(1024)(128)(2,1)S(1)}, bf16[768]{0:T(1024)(128)(2,1)S(1)}, bf16[768]{0:T(1024)(128)(2,1)S(1)}, bf16[768]{0:T(1024)(128)(2,1)S(1)}, bf16[768]{0:T(1024)(128)(2,1)S(1)}) all-reduce(bf16[768]{0:T(1024)(128)(2,1)S(1)} %dynamic-update-slice.1, ...), channel_id=1, replica_groups=mesh['fsdp'=4,'ctx'=8] {'fsdp'}, use_global_device_ids=true, to_apply=%add.1 | all-reduce | flops 3840 | bytes 15360
  36.9 6.5 all-gather.11.cloned.1.call-done
  52.3 5.2 all-gather.3
  59.9 31.3 %all-gather.19.cloned.1.call-done = bf16[1024,768]{1,0:T(8,128)(2,1)} async-done(((bf16[128,768]{1,0:T(8,128)(2,1)}), bf16[1024,768]{1,0:T(8,128)(2,1)}) %all-gather.19.cloned.1.call-update) | async-done | bytes 1572880 | tf_op jit(solution)/shard_map/all_gather | solution.py:146
  91.2 45.3 %all-gather.21.cloned.1.call-done = bf16[1024,768]{1,0:T(8,128)(2,1)} async-done(((bf16[128,768]{1,0:T(8,128)(2,1)}), bf16[1024,768]{1,0:T(8,128)(2,1)}) %all-gather.21.cloned.1.call-update) | async-done | bytes 1572880 | tf_op jit(solution)/shard_map/all_gather | solution.py:147
  136.5 14.1 %conditional.2 = (f32[1,12,128]{2,1,0:T(8,128)S(1)}, f32[1,12,128]{2,1,0:T(8,128)S(1)}, f32[1,128,12,64]{1,3,2,0:T(8,128)S(1)}) conditional(s32[]{:T(128)} %convert_element_type.236, (f32[1,12,128]{2,1,0:T(8,128)S(1)}, f32[1,12,128]{2,1,0:T(8,128)S(1)}, f32[1,128,12,64]{1,3,2,0:T(8,128)S(1)}) %tuple.49, (pred[1,128,1024]{2,1,0:T(8,128)(4,1)S(1)}, ...), branch_computations={%region_3.4_spmd, %region_4.7_spmd} | conditional | flops 423301632 | bytes 62464332 | solution.py:178
  145.3 5.2 fusion.13
  156.3 36.4 %all-gather.15.cloned.1.call-done = bf16[768,3072]{1,0:T(8,128)(2,1)} async-done(((bf16[192,3072]{1,0:T(8,128)(2,1)}), bf16[768,3072]{1,0:T(8,128)(2,1)}) %all-gather.15.cloned.1.call-update) | async-done | bytes 4718608 | tf_op jit(solution)/shard_map/all_gather | solution.py:102
  195.9 35.6 %all-gather.17.cloned.1.call-done = bf16[3072,768]{1,0:T(8,128)(2,1)} async-done(((bf16[768,768]{1,0:T(8,128)(2,1)}), bf16[3072,768]{1,0:T(8,128)(2,1)}) %all-gather.17.cloned.1.call-update) | async-done | bytes 4718608 | tf_op jit(solution)/shard_map/all_gather | solution.py:104
  231.6 5.5 fusion.105
  246.2 182.5 %while.34 = (s32[]{:T(128)}, f32[1,128,12,64]{1,3,2,0:T(8,128)S(1)}, bf16[1,128,768]{1,2,0:T(8,128)(2,1)S(1)}, bf16[1,128,768]{1,2,0:T(8,128)(2,1)S(1)}, f32[1,1...) while((s32[]{:T(128)}, ...), condition=%wide.region_16.17_spmd.clone.clone.clone, body=%wide.region_12.16_spmd.clone.clone.clone.sunk | while | flops 128363792 | bytes 15187074 | solution.py:279
  275.0 8.4 collective-permute-start.2
  297.8 8.4 collective-permute-start.2
  306.4 5.1 collective-permute-done.2
  320.8 8.4 collective-permute-start.2
  342.9 8.4 collective-permute-start.2
  366.2 8.4 collective-permute-start.2
  388.7 8.4 collective-permute-start.2
  410.4 8.4 collective-permute-start.2
  449.7 32.8 %all-reduce.15 = (bf16[768]{0:T(1024)(128)(2,1)S(1)}, bf16[768]{0:T(1024)(128)(2,1)S(1)}, bf16[768]{0:T(1024)(128)(2,1)S(1)}, bf16[1536]{0:T(1024)(128)(2,1)S(1)...) all-reduce(bf16[768]{0:T(1024)(128)(2,1)} %copy-done.46, ...), channel_id=1, replica_groups=mesh['fsdp'=4,'ctx'=8] {'fsdp'}, use_global_device_ids=true, to_apply=%add.5 | all-reduce | flops 9984 | bytes 39936
  493.7 50.5 %reduce-scatter.9.cloned.1.call-done = bf16[192,3072]{1,0:T(8,128)(2,1)} async-done(((bf16[768,3072]{1,0:T(8,128)(2,1)}), bf16[192,3072]{1,0:T(8,128)(2,1)}) %reduce-scatter.9.cloned.1.call-update) | async-done | bytes 1179664 | tf_op jit(solution)/shard_map/reduce_scatter | solution.py:332
  544.2 50.4 %reduce-scatter.11.cloned.1.call-done = bf16[768,768]{1,0:T(8,128)(2,1)} async-done(((bf16[3072,768]{1,0:T(8,128)(2,1)}), bf16[768,768]{1,0:T(8,128)(2,1)}) %reduce-scatter.11.cloned.1.call-update) | async-done | bytes 1179664 | tf_op jit(solution)/shard_map/reduce_scatter | solution.py:338
  594.6 278.9 %all-reduce.18 = (f32[192]{0:T(256)}, f32[192]{0:T(256)}, f32[192,2304]{1,0:T(8,128)}, f32[384]{0:T(512)}, f32[192,768]{1,0:T(8,128)}, /*index=5*/f32[192]{0:T(2...) all-reduce(f32[192]{0:T(256)S(1)} %dynamic-slice_convert_fusion.7, ...), channel_id=1, replica_groups=mesh['fsdp'=4,'ctx'=8] {'ctx'}, use_global_device_ids=true, to_apply=%region_21.22 | all-reduce | flops 1771776 | bytes 10635264 | tf_op jit(solution)/shard_map/psum | solution.py:345
  (376 shorter events, 191.9 us)
Async XLA Ops:
  7.2 36.1 %all-gather.11.cloned.1.call-start = ((), (), s32[]{:S(2)}) async-start(), calls=%async_computation.4 | async-start | bytes 4423680 | tf_op jit(solution)/shard_map/all_gather | solution.py:96
  7.9 83.3 %all-gather.19.cloned.1.call-start = ((), (), s32[]{:S(2)}) async-start(), calls=%async_computation.12 | async-start | bytes 1769472 | tf_op jit(solution)/shard_map/all_gather | solution.py:146
  46.9 89.7 %all-gather.21.cloned.1.call-start = ((), (), s32[]{:S(2)}) async-start(), calls=%async_computation.13 | async-start | bytes 1769472 | tf_op jit(solution)/shard_map/all_gather | solution.py:147
  47.6 106.2 %all-gather.13.cloned.1.call-start = ((), (), s32[]{:S(2)}) async-start(), calls=%async_computation.5 | async-start | bytes 1474560 | tf_op jit(solution)/shard_map/all_gather | solution.py:98
  48.2 144.5 %all-gather.15.cloned.1.call-start = ((), (), s32[]{:S(2)}) async-start(), calls=%async_computation.6 | async-start | bytes 5898240 | tf_op jit(solution)/shard_map/all_gather | solution.py:102
  48.8 182.8 %all-gather.17.cloned.1.call-start = ((), (), s32[]{:S(2)}) async-start(), calls=%async_computation.7 | async-start | bytes 5898240 | tf_op jit(solution)/shard_map/all_gather | solution.py:104
  49.4 440.5 %reduce-scatter.7.cloned.1.call-start = ((), (), s32[]{:S(2)}) async-start(), calls=%async_computation.9 | async-start | bytes 1474560 | tf_op jit(solution)/shard_map/reduce_scatter | solution.py:320
  246.1 247.6 %reduce-scatter.5.cloned.1.call-start = ((), (), s32[]{:S(2)}) async-start(), calls=%async_computation.8 | async-start | bytes 4423680 | tf_op jit(solution)/shard_map/reduce_scatter | solution.py:314
  252.3 9.6 %collective-permute-start.2 = (bf16[1,128,12,64]{1,3,2,0:T(8,128)(2,1)S(1)}, bf16[1,128,12,64]{1,3,2,0:T(8,128)(2,1)S(1)}, u32[]{:S(2)}, u32[]{:S(2)}) collective-permute-start(bf16[1,128,12,64]{1,3,2,0:T(8,128)(2,1)S(1)} %convert_element_type.408), channel_id=1, source_target_pairs={{0,7},{1,0},{2,1},{3,2},{4,3},{5,4},{6,5},{7,6},{8,15},{9,8},{10,9... | collective-permute-start | bytes 589832 | tf_op jit(solution)/shard_map/while/body/eval_jaxpr/ppermute | solution.py:17
  257.2 12.7 %collective-permute-start = (bf16[1,128,768]{1,2,0:T(8,128)(2,1)S(1)}, bf16[1,128,768]{1,2,0:T(8,128)(2,1)S(1)}, u32[]{:S(2)}, u32[]{:S(2)}) collective-permute-start(bf16[1,128,768]{1,2,0:T(8,128)(2,1)S(1)} %copy.75), channel_id=1, source_target_pairs={{0,7},{1,0},{2,1},{3,2},{4,3},{5,4},{6,5},{7,6},{8,15},{9,8},{10,9... | collective-permute-start | bytes 589832 | tf_op jit(solution)/shard_map/while/body/eval_jaxpr/ppermute | solution.py:17
  258.7 13.4 %collective-permute-start.1 = (bf16[1,128,768]{1,2,0:T(8,128)(2,1)S(1)}, bf16[1,128,768]{1,2,0:T(8,128)(2,1)S(1)}, u32[]{:S(2)}, u32[]{:S(2)}) collective-permute-start(bf16[1,128,768]{1,2,0:T(8,128)(2,1)S(1)} %copy.76), channel_id=1, source_target_pairs={{0,7},{1,0},{2,1},{3,2},{4,3},{5,4},{6,5},{7,6},{8,15},{9,8},{10,9... | collective-permute-start | bytes 589832 | tf_op jit(solution)/shard_map/while/body/eval_jaxpr/ppermute | solution.py:17
  275.0 13.5 %collective-permute-start.2 = (bf16[1,128,12,64]{1,3,2,0:T(8,128)(2,1)S(1)}, bf16[1,128,12,64]{1,3,2,0:T(8,128)(2,1)S(1)}, u32[]{:S(2)}, u32[]{:S(2)}) collective-permute-start(bf16[1,128,12,64]{1,3,2,0:T(8,128)(2,1)S(1)} %convert_element_type.408), channel_id=1, source_target_pairs={{0,7},{1,0},{2,1},{3,2},{4,3},{5,4},{6,5},{7,6},{8,15},{9,8},{10,9... | collective-permute-start | bytes 589832 | tf_op jit(solution)/shard_map/while/body/eval_jaxpr/ppermute | solution.py:17
  283.5 11.3 %collective-permute-start.1 = (bf16[1,128,768]{1,2,0:T(8,128)(2,1)S(1)}, bf16[1,128,768]{1,2,0:T(8,128)(2,1)S(1)}, u32[]{:S(2)}, u32[]{:S(2)}) collective-permute-start(bf16[1,128,768]{1,2,0:T(8,128)(2,1)S(1)} %copy.76), channel_id=1, source_target_pairs={{0,7},{1,0},{2,1},{3,2},{4,3},{5,4},{6,5},{7,6},{8,15},{9,8},{10,9... | collective-permute-start | bytes 589832 | tf_op jit(solution)/shard_map/while/body/eval_jaxpr/ppermute | solution.py:17
  297.8 13.7 %collective-permute-start.2 = (bf16[1,128,12,64]{1,3,2,0:T(8,128)(2,1)S(1)}, bf16[1,128,12,64]{1,3,2,0:T(8,128)(2,1)S(1)}, u32[]{:S(2)}, u32[]{:S(2)}) collective-permute-start(bf16[1,128,12,64]{1,3,2,0:T(8,128)(2,1)S(1)} %convert_element_type.408), channel_id=1, source_target_pairs={{0,7},{1,0},{2,1},{3,2},{4,3},{5,4},{6,5},{7,6},{8,15},{9,8},{10,9... | collective-permute-start | bytes 589832 | tf_op jit(solution)/shard_map/while/body/eval_jaxpr/ppermute | solution.py:17
  306.3 11.5 %collective-permute-start.1 = (bf16[1,128,768]{1,2,0:T(8,128)(2,1)S(1)}, bf16[1,128,768]{1,2,0:T(8,128)(2,1)S(1)}, u32[]{:S(2)}, u32[]{:S(2)}) collective-permute-start(bf16[1,128,768]{1,2,0:T(8,128)(2,1)S(1)} %copy.76), channel_id=1, source_target_pairs={{0,7},{1,0},{2,1},{3,2},{4,3},{5,4},{6,5},{7,6},{8,15},{9,8},{10,9... | collective-permute-start | bytes 589832 | tf_op jit(solution)/shard_map/while/body/eval_jaxpr/ppermute | solution.py:17
  320.8 12.8 %collective-permute-start.2 = (bf16[1,128,12,64]{1,3,2,0:T(8,128)(2,1)S(1)}, bf16[1,128,12,64]{1,3,2,0:T(8,128)(2,1)S(1)}, u32[]{:S(2)}, u32[]{:S(2)}) collective-permute-start(bf16[1,128,12,64]{1,3,2,0:T(8,128)(2,1)S(1)} %convert_element_type.408), channel_id=1, source_target_pairs={{0,7},{1,0},{2,1},{3,2},{4,3},{5,4},{6,5},{7,6},{8,15},{9,8},{10,9... | collective-permute-start | bytes 589832 | tf_op jit(solution)/shard_map/while/body/eval_jaxpr/ppermute | solution.py:17
  330.0 9.9 %collective-permute-start.1 = (bf16[1,128,768]{1,2,0:T(8,128)(2,1)S(1)}, bf16[1,128,768]{1,2,0:T(8,128)(2,1)S(1)}, u32[]{:S(2)}, u32[]{:S(2)}) collective-permute-start(bf16[1,128,768]{1,2,0:T(8,128)(2,1)S(1)} %copy.76), channel_id=1, source_target_pairs={{0,7},{1,0},{2,1},{3,2},{4,3},{5,4},{6,5},{7,6},{8,15},{9,8},{10,9... | collective-permute-start | bytes 589832 | tf_op jit(solution)/shard_map/while/body/eval_jaxpr/ppermute | solution.py:17
  342.9 13.7 %collective-permute-start.2 = (bf16[1,128,12,64]{1,3,2,0:T(8,128)(2,1)S(1)}, bf16[1,128,12,64]{1,3,2,0:T(8,128)(2,1)S(1)}, u32[]{:S(2)}, u32[]{:S(2)}) collective-permute-start(bf16[1,128,12,64]{1,3,2,0:T(8,128)(2,1)S(1)} %convert_element_type.408), channel_id=1, source_target_pairs={{0,7},{1,0},{2,1},{3,2},{4,3},{5,4},{6,5},{7,6},{8,15},{9,8},{10,9... | collective-permute-start | bytes 589832 | tf_op jit(solution)/shard_map/while/body/eval_jaxpr/ppermute | solution.py:17
  351.4 9.8 %collective-permute-start = (bf16[1,128,768]{1,2,0:T(8,128)(2,1)S(1)}, bf16[1,128,768]{1,2,0:T(8,128)(2,1)S(1)}, u32[]{:S(2)}, u32[]{:S(2)}) collective-permute-start(bf16[1,128,768]{1,2,0:T(8,128)(2,1)S(1)} %copy.75), channel_id=1, source_target_pairs={{0,7},{1,0},{2,1},{3,2},{4,3},{5,4},{6,5},{7,6},{8,15},{9,8},{10,9... | collective-permute-start | bytes 589832 | tf_op jit(solution)/shard_map/while/body/eval_jaxpr/ppermute | solution.py:17
  366.2 13.2 %collective-permute-start.2 = (bf16[1,128,12,64]{1,3,2,0:T(8,128)(2,1)S(1)}, bf16[1,128,12,64]{1,3,2,0:T(8,128)(2,1)S(1)}, u32[]{:S(2)}, u32[]{:S(2)}) collective-permute-start(bf16[1,128,12,64]{1,3,2,0:T(8,128)(2,1)S(1)} %convert_element_type.408), channel_id=1, source_target_pairs={{0,7},{1,0},{2,1},{3,2},{4,3},{5,4},{6,5},{7,6},{8,15},{9,8},{10,9... | collective-permute-start | bytes 589832 | tf_op jit(solution)/shard_map/while/body/eval_jaxpr/ppermute | solution.py:17
  388.7 12.4 %collective-permute-start.2 = (bf16[1,128,12,64]{1,3,2,0:T(8,128)(2,1)S(1)}, bf16[1,128,12,64]{1,3,2,0:T(8,128)(2,1)S(1)}, u32[]{:S(2)}, u32[]{:S(2)}) collective-permute-start(bf16[1,128,12,64]{1,3,2,0:T(8,128)(2,1)S(1)} %convert_element_type.408), channel_id=1, source_target_pairs={{0,7},{1,0},{2,1},{3,2},{4,3},{5,4},{6,5},{7,6},{8,15},{9,8},{10,9... | collective-permute-start | bytes 589832 | tf_op jit(solution)/shard_map/while/body/eval_jaxpr/ppermute | solution.py:17
  410.4 11.6 %collective-permute-start.2 = (bf16[1,128,12,64]{1,3,2,0:T(8,128)(2,1)S(1)}, bf16[1,128,12,64]{1,3,2,0:T(8,128)(2,1)S(1)}, u32[]{:S(2)}, u32[]{:S(2)}) collective-permute-start(bf16[1,128,12,64]{1,3,2,0:T(8,128)(2,1)S(1)} %convert_element_type.408), channel_id=1, source_target_pairs={{0,7},{1,0},{2,1},{3,2},{4,3},{5,4},{6,5},{7,6},{8,15},{9,8},{10,9... | collective-permute-start | bytes 589832 | tf_op jit(solution)/shard_map/while/body/eval_jaxpr/ppermute | solution.py:17
  432.5 111.7 %reduce-scatter.9.cloned.1.call-start = ((), (), s32[]{:S(2)}) async-start(), calls=%async_computation.10 | async-start | bytes 5898240 | tf_op jit(solution)/shard_map/reduce_scatter | solution.py:332
  437.3 157.3 %reduce-scatter.11.cloned.1.call-start = ((), (), s32[]{:S(2)}) async-start(), calls=%async_computation.11 | async-start | bytes 5898240 | tf_op jit(solution)/shard_map/reduce_scatter | solution.py:338
  (67 other events, 779.0 us)
Sparse Core Ops, SparseCore 0:
  9.6 33.7 all-gather.10
  47.0 44.1 all-gather.18
  94.0 42.5 all-gather.20
  138.0 15.8 all-gather.12
  155.2 37.4 all-gather.14
  194.1 37.4 all-gather.16
  246.2 25.5 reduce-scatter.6
  432.6 61.0 reduce-scatter.4
  496.3 47.9 reduce-scatter.8
  546.6 47.9 reduce-scatter.10
where the time goes:
time: 883 us; the launch traced here: 880 us
  waiting for transfers between devices  340 us (39%)
  blocking collectives  337 us (38%)
  starting transfers between devices  79.5 us (9%)
  matrix products  47.7 us (5%)
  other arithmetic  33.8 us (4%)
  between operations  18.5 us (2%)
  local copies, waits for them, and re-layouts  18 us (2%)
    psum x1, blocking collectives, body(): lax.psum((owned_all[0], owned_all[1], owned_all[2], owned_all[3], owned_a...  279 us
    ppermute x32, starting transfers between devices, from_behind(): return lax.ppermute(x, axis, [(i, (i + by) % count) for i in range(count)])  78.8 us
    ppermute x32, waiting for transfers between devices, from_behind(): return lax.ppermute(x, axis, [(i, (i + by) % count) for i in range(count)])  76.1 us
    reduce_scatter x1, waiting for transfers between devices, body(): lax.psum_scatter(grad_fc.astype(jnp.bfloat16), 'fsdp', scatter_dimension=...  50.5 us
    reduce_scatter x1, waiting for transfers between devices, body(): lax.psum_scatter(grad_proj.astype(jnp.bfloat16), 'fsdp', scatter_dimensio...  50.4 us
    unnamed x2, blocking collectives  46.3 us
    all_gather x1, waiting for transfers between devices, body(): lax.all_gather(values_own, 'ctx', axis=1, tiled=True)  45.3 us
    all_gather x1, waiting for transfers between devices, body(): lax.all_gather(fc_weight, 'fsdp', axis=0, tiled=True)  36.4 us
  transfers between devices with their start and end apart: 42, of which 41 were waited for; matrix products, arithmetic and copies ran while one was open for 9% of the time, Pallas kernels for 0%

commit v1 on v0

v1 whole, which is shorter than its diff:
```python
import jax
import jax.numpy as jnp
from jax import lax
from jax.experimental import pallas as pl
from jax.experimental.pallas import tpu as pltpu
from jax.sharding import PartitionSpec as P

HD = 64
EPSILON = 1e-05
NEGATIVE = -1e30
GELU_COEF = 0.7978845608028654
CUBE = 0.044715
F32 = jnp.float32
BF16 = jnp.bfloat16
WAYS = 4
PIECES = 8


def f_xor(x, k):
    n = lax.axis_size("fsdp")
    return lax.ppermute(x, "fsdp", [(i, i ^ k) for i in range(n)])


def c_xor(x, k):
    n = lax.axis_size("ctx")
    return lax.ppermute(x, "ctx", [(i, i ^ k) for i in range(n)])


def swap_layout(x):
    group = lax.axis_size("ctx")
    members = group // WAYS
    perm = []
    for f in range(WAYS):
        for c in range(group):
            j, m = divmod(c, members)
            perm.append((f * group + c, j * group + f * members + m))
    return lax.ppermute(x, ("fsdp", "ctx"), perm)


def gather_f(x):
    far = f_xor(x, 2)
    near = f_xor(x, 1)
    return [x, near, far, f_xor(far, 1)]


def scatter_f(kept_own, kept_far, sent):
    got = f_xor(sent, 1)
    far = (kept_far + got[1].astype(F32)).astype(BF16)
    return kept_own, got, f_xor(far, 2)


def reduce_c(slots):
    group = lax.axis_size("ctx")
    value = slots
    for bit in range(3):
        half = value.shape[0] // 2
        got = c_xor(value[half:], 1 << bit)
        value = (value[:half].astype(F32) + got.astype(F32)).astype(BF16)
    value = value[0]
    bit = 3
    while (1 << bit) < group:
        value = (value.astype(F32) + c_xor(value, 1 << bit).astype(F32)).astype(BF16)
        bit += 1
    return value


def gather_c(value):
    value = value[None]
    for bit in (2, 1, 0):
        value = jnp.concatenate([value, c_xor(value, 1 << bit)], axis=0)
    return value


def sum_all(rows):
    for k in (1, 2):
        rows = rows + f_xor(rows, k)
    k = 1
    while k < lax.axis_size("ctx"):
        rows = rows + c_xor(rows, k)
        k *= 2
    return rows


def call(kernel, outs, args, scratch=(), flops=0, name=None):
    vmem = pl.BlockSpec(memory_space=pltpu.VMEM)
    moved = sum(a.size * a.dtype.itemsize for a in args) + sum(
        o.size * o.dtype.itemsize for o in outs
    )
    return pl.pallas_call(
        kernel,
        out_shape=tuple(outs),
        in_specs=[pl.BlockSpec(memory_space=pltpu.SMEM)] + [vmem] * (len(args) - 1),
        out_specs=tuple([vmem] * len(outs)),
        scratch_shapes=list(scratch),
        cost_estimate=pl.CostEstimate(flops=flops, bytes_accessed=moved, transcendentals=0),
        compiler_params=pltpu.CompilerParams(vmem_limit_bytes=48 * 1024 * 1024),
        name=name,
    )(*args)


def shape(dims, dtype):
    return jax.ShapeDtypeStruct(dims, dtype)


def dot(a, b, contract):
    return lax.dot_general(a, b, ((contract[0:1], contract[1:2]), ((), ())), preferred_element_type=F32)


def block_rows(index, size):
    return pl.ds(pl.multiple_of(index * size, size), size)


def normalise(values):
    centred = values - jnp.mean(values, axis=-1, keepdims=True)
    inverse = lax.rsqrt(jnp.mean(centred * centred, axis=-1, keepdims=True) + EPSILON)
    return centred * inverse, inverse


def norm_back(upstream, scaled, inverse, gain):
    weighted = upstream * gain
    return inverse * (
        weighted
        - jnp.mean(weighted, axis=-1, keepdims=True)
        - scaled * jnp.mean(weighted * scaled, axis=-1, keepdims=True)
    )


def valid_rows(sc, chunk, rows):
    place = (chunk * sc[3] + sc[2]) * rows + lax.broadcasted_iota(jnp.int32, (rows, 1), 0)
    return place < sc[4]


def emit_partials(sc, rows, value_ref, own_ref, far_ref, sent_ref):
    f = sc[0]
    own_ref[...] = value_ref[block_rows(f, rows), :]
    far_ref[...] = value_ref[block_rows(f ^ 2, rows), :]
    sent_ref[0] = value_ref[block_rows(f ^ 1, rows), :].astype(BF16)
    sent_ref[1] = value_ref[block_rows(f ^ 3, rows), :].astype(BF16)


def cot_kernel(sc, c0, c1, c2, c3, proj, g_out, pulled, bias_row):
    rows = c0.shape[0]
    for k, ref in enumerate((c0, c1, c2, c3)):
        j = sc[0] ^ k
        kept = jnp.where(valid_rows(sc, j, rows), ref[...].astype(F32), 0.0)
        if k == 0:
            bias_row[...] = jnp.sum(kept, axis=0, keepdims=True)
        low = kept.astype(BF16)
        g_out[block_rows(j, rows), :] = low
        pulled[block_rows(j, rows), :] = dot(low, proj[...], (1, 1))


def qkv_kernel(sc, x0, x1, x2, x3, w0, w1, w2, w3, table, bias, normed, full, q, kv):
    rows, wrows = x0.shape[0], w0.shape[0]
    for k, ref in enumerate((w0, w1, w2, w3)):
        full[block_rows(sc[0] ^ k, wrows), :] = ref[...]
    for k, ref in enumerate((x0, x1, x2, x3)):
        place = block_rows(sc[0] ^ k, rows)
        scaled, _ = normalise(ref[...].astype(F32))
        low = (scaled * table[0:1, :] + table[1:2, :]).astype(BF16)
        normed[place, :] = low
        got = (dot(low, full[...], (1, 0)) + bias[...]).astype(BF16)
        width = q.shape[1]
        q[place, :] = got[:, :width] * jnp.asarray(0.125, BF16)
        kv[place, :] = got[:, width:]


def split3(value):
    high = value.astype(BF16)
    rest = value - high.astype(F32)
    mid = rest.astype(BF16)
    low = (rest - mid.astype(F32)).astype(BF16)
    return high, mid, low


def lanes(columns, rows, width, dtype):
    lane = lax.broadcasted_iota(jnp.int32, (rows, width), 1)
    out = jnp.zeros((rows, width), F32)
    for i, column in enumerate(columns):
        out = jnp.where(lane == i, column.astype(F32), out)
    return out.astype(dtype)


def joined(ref, base, count, h):
    total = None
    for part in range(3):
        column = base + part * count + h
        piece = ref[:, column : column + 1].astype(F32)
        total = piece if total is None else total + piece
    return total


def threshold(sc, other):
    return jnp.where(other == sc[2], 0, jnp.where(other < sc[2], 1 << 20, -(1 << 20)))


def attend(sc, step, first, last, refs):
    if first:
        q, kv = refs[:2]
        state_in = None
        rest = refs[2:]
    else:
        q, kv, acc_in, stat_in = refs[:4]
        rest = refs[4:]
    if last:
        out_w, attended, low, q_ext, own, far, sent, scratch = rest
    else:
        acc_out, stat_out = rest
    total, width = q.shape
    rows = total // WAYS
    heads = width // HD
    limit = threshold(sc, sc[2] ^ step)
    ahead = lax.broadcasted_iota(jnp.int32, (rows, rows), 1) - lax.broadcasted_iota(
        jnp.int32, (rows, rows), 0
    )
    allowed = ahead <= limit
    for jq in range(WAYS):
        place = slice(jq * rows, (jq + 1) * rows)
        parts, tops, sums = [], [], []
        for h in range(heads):
            cols = slice(h * HD, (h + 1) * HD)
            vcols = slice(width + h * HD, width + (h + 1) * HD)
            qh = q[place, cols]
            diag = jnp.where(allowed, dot(qh, kv[place, cols], (1, 1)), NEGATIVE)
            top = jnp.max(diag, axis=-1, keepdims=True)
            if jq > 0:
                before = dot(qh, kv[: jq * rows, cols], (1, 1))
                top = jnp.maximum(top, jnp.max(before, axis=-1, keepdims=True))
            if not first:
                old = stat_in[place, h : h + 1]
                top = jnp.maximum(top, old)
            weight = jnp.exp(diag - top)
            count = jnp.sum(weight, axis=-1, keepdims=True)
            acc = dot(weight.astype(BF16), kv[place, vcols], (1, 0))
            if jq > 0:
                weight = jnp.exp(before - top)
                count = count + jnp.sum(weight, axis=-1, keepdims=True)
                acc = acc + dot(weight.astype(BF16), kv[: jq * rows, vcols], (1, 0))
            if not first:
                shrink = jnp.exp(old - top)
                count = count + shrink * stat_in[place, heads + h : heads + h + 1]
                acc = acc + shrink * acc_in[place, cols]
            if last:
                acc = acc / count
                tops.append(top + jnp.log(count))
            else:
                tops.append(top)
                sums.append(count)
            parts.append(acc)
        joined_parts = jnp.concatenate(parts, axis=1)
        if last:
            attended[place, :] = joined_parts
            low_part = joined_parts.astype(BF16)
            low[place, :] = low_part
            scratch[place, :] = dot(low_part, out_w[...], (1, 0))
            split = [split3(t) for t in tops]
            columns = [split[h][part] for part in range(3) for h in range(heads)]
            q_ext[place, :width] = q[place, :]
            q_ext[place, width:] = lanes(columns, rows, q_ext.shape[1] - width, BF16)
        else:
            acc_out[place, :] = joined_parts
            stat_out[place, :] = lanes(tops + sums, rows, stat_out.shape[1], F32)
    if last:
        emit_partials(sc, rows, scratch, own, far, sent)


def second_norm_kernel(sc, own, got, far, x, table, residual, normed):
    value = (
        x[...].astype(F32)
        + own[...]
        + got[0].astype(F32)
        + far[...].astype(F32)
        + table[2:3, :]
    )
    residual[...] = value
    scaled, _ = normalise(value)
    normed[...] = (scaled * table[3:4, :] + table[4:5, :]).astype(BF16)


def feed_kernel(
    sc, n0, n1, n2, n3, w0, w1, w2, w3, bias, pulled,
    normed, full, active, g_hidden, bias_row, own, far, sent, scratch,
):
    rows, wrows = n0.shape[0], w0.shape[0]
    for k, ref in enumerate((w0, w1, w2, w3)):
        full[block_rows(sc[0] ^ k, wrows), :] = ref[...]
    total = jnp.zeros_like(bias_row)
    for k, ref in enumerate((n0, n1, n2, n3)):
        place = block_rows(sc[0] ^ k, rows)
        normed[place, :] = ref[...]
        hidden = dot(ref[...], full[...], (1, 0)) + bias[...]
        square = hidden * hidden
        bend = jnp.tanh(GELU_COEF * (hidden + CUBE * hidden * square))
        active[place, :] = (0.5 * hidden * (1.0 + bend)).astype(BF16)
        slope = 0.5 * (1.0 + bend) + 0.5 * hidden * (1.0 - bend * bend) * (
            GELU_COEF * (1.0 + 3.0 * CUBE * square)
        )
        low = (pulled[place, :] * slope).astype(BF16)
        g_hidden[place, :] = low
        total = total + jnp.sum(low.astype(F32), axis=0, keepdims=True)
        scratch[place, :] = dot(low, full[...], (1, 1))
    bias_row[...] = total
    emit_partials(sc, rows, scratch, own, far, sent)


def result_kernel(sc, active, proj, own, far, sent, scratch):
    rows = active.shape[0] // WAYS
    scratch[...] = dot(active[...], proj[...], (1, 0))
    emit_partials(sc, rows, scratch, own, far, sent)


def reverse(r):
    return ((r & 1) << 2) | (r & 2) | (r >> 2)


def slot_of(sc, piece):
    return reverse((sc[1] ^ piece) & 7)


def feed_grad_kernel(sc, active, g_out, normed, g_hidden, slots):
    step_rows, step_cols = slots.shape[2], slots.shape[3]
    quarter = step_rows // WAYS
    for a in range(WAYS):
        wide = dot(active[:, a * step_rows : (a + 1) * step_rows], g_out[...], (0, 0)).astype(BF16)
        for b in range(2):
            slots[slot_of(sc, a * 2 + b), 0] = wide[:, b * step_cols : (b + 1) * step_cols]
    for fp in range(WAYS):
        wide = dot(normed[:, fp * step_rows : (fp + 1) * step_rows], g_hidden[...], (0, 0)).astype(BF16)
        for a in range(WAYS):
            for b in range(2):
                slots[slot_of(sc, a * 2 + b), 1, block_rows(sc[0] ^ fp, quarter), :] = wide[
                    a * quarter : (a + 1) * quarter, b * step_cols : (b + 1) * step_cols
                ]


def second_back_kernel(sc, own, got, far, residual, cot, table, g_residual, g_branch, rows_out):
    upstream = own[...] + got[0].astype(F32) + far[...].astype(F32)
    scaled, inverse = normalise(residual[...])
    through = norm_back(upstream, scaled, inverse, table[3:4, :])
    g_out = jnp.where(valid_rows(sc, sc[0], cot.shape[0]), cot[...].astype(F32), 0.0)
    value = g_out + through
    g_residual[...] = value
    low = value.astype(BF16)
    g_branch[...] = low
    rows_out[0:1, :] = jnp.sum(upstream * scaled, axis=0, keepdims=True)
    rows_out[1:2, :] = jnp.sum(upstream, axis=0, keepdims=True)
    rows_out[2:3, :] = jnp.sum(low.astype(F32), axis=0, keepdims=True)


def pull_kernel(sc, b0, b1, b2, b3, out_w, attended, g_branch, do_ext):
    rows = b0.shape[0]
    width = attended.shape[1]
    heads = width // HD
    for k, ref in enumerate((b0, b1, b2, b3)):
        place = block_rows(sc[0] ^ k, rows)
        g_branch[place, :] = ref[...]
        low = dot(ref[...], out_w[...], (1, 1)).astype(BF16)
        product = low.astype(F32) * attended[place, :]
        split = [
            split3(jnp.sum(product[:, h * HD : (h + 1) * HD], axis=-1, keepdims=True))
            for h in range(heads)
        ]
        columns = [split[h][part] for part in range(3) for h in range(heads)]
        do_ext[place, :width] = low
        do_ext[place, width:] = lanes(columns, rows, do_ext.shape[1] - width, BF16)


def out_grad_kernel(sc, low, g_branch, slots):
    step_rows, step_cols = slots.shape[1], slots.shape[2]
    wide = dot(low[...], g_branch[...], (0, 0)).astype(BF16)
    for a in range(WAYS):
        for b in range(2):
            slots[slot_of(sc, a * 2 + b)] = wide[
                a * step_rows : (a + 1) * step_rows, b * step_cols : (b + 1) * step_cols
            ]


def pair_back(q, do, kv, allowed, want_q, want_kv, g_q, g_kv, start):
    total = kv.shape[0]
    width = kv.shape[1] // 2
    rows = total // WAYS
    heads = width // HD
    if start and want_kv:
        g_kv[...] = jnp.zeros_like(g_kv)
    for jq in range(WAYS):
        place = slice(jq * rows, (jq + 1) * rows)
        tail_q = q[place, width:].astype(F32)
        tail_do = do[place, width:].astype(F32)
        for h in range(heads):
            cols = slice(h * HD, (h + 1) * HD)
            vcols = slice(width + h * HD, width + (h + 1) * HD)
            qh = q[place, cols]
            doh = do[place, cols]
            pick = lambda t: (
                t[:, h : h + 1] + t[:, heads + h : heads + h + 1]
            ) + t[:, 2 * heads + h : 2 * heads + h + 1]
            lse, delta = pick(tail_q), pick(tail_do)
            grad = None
            for diag in ((True, False) if jq > 0 else (True,)):
                keys = place if diag else slice(0, jq * rows)
                scores = dot(qh, kv[keys, cols], (1, 1))
                weight = jnp.exp(scores - lse)
                if diag:
                    weight = jnp.where(allowed, weight, 0.0)
                pulled = dot(doh, kv[keys, vcols], (1, 1))
                low = (weight * (pulled - delta)).astype(BF16)
                if want_q:
                    more = dot(low, kv[keys, cols], (1, 0))
                    grad = more if grad is None else grad + more
                if want_kv:
                    g_kv[keys, cols] += dot(low, qh, (0, 0))
                    g_kv[keys, vcols] += dot(weight.astype(BF16), doh, (0, 0))
            if want_q:
                if start:
                    g_q[place, cols] = grad
                else:
                    g_q[place, cols] += grad


def back_first(sc, q, do, kv, g_q, g_kv):
    rows = kv.shape[0] // WAYS
    ahead = lax.broadcasted_iota(jnp.int32, (rows, rows), 1) - lax.broadcasted_iota(
        jnp.int32, (rows, rows), 0
    )
    pair_back(q, do, kv, ahead <= 0, True, True, g_q, g_kv, True)


def back_step(sc, step, last, refs):
    q, do, kv, q_other, do_other, kv_other, q_in, kv_in = refs[:8]
    if last:
        full, g_proj, own, far, sent, g_q, g_kv, scratch = refs[8:]
    else:
        g_q, g_kv = refs[8:]
    total = kv.shape[0]
    width = kv.shape[1] // 2
    rows = total // WAYS
    other = sc[2] ^ step
    ahead = jnp.zeros((rows, rows), jnp.int32)
    g_q[...] = q_in[...]
    g_kv[...] = kv_in[...]
    pair_back(q, do, kv_other, ahead <= jnp.where(other < sc[2], 1, -1), True, False, g_q, g_kv, False)
    pair_back(q_other, do_other, kv, ahead <= jnp.where(sc[2] < other, 1, -1), False, True, g_q, g_kv, False)
    if last:
        g_proj[:, :width] = (g_q[...] * 0.125).astype(BF16)
        g_proj[:, width:] = g_kv[...].astype(BF16)
        scratch[...] = dot(g_proj[...], full[...], (1, 1))
        emit_partials(sc, rows, scratch, own, far, sent)


def qkv_grad_kernel(sc, normed, g_proj, slots, sums):
    step = slots.shape[2]
    wrows = step * PIECES
    for fp in range(WAYS):
        wide = dot(normed[:, fp * wrows : (fp + 1) * wrows], g_proj[...], (0, 0)).astype(BF16)
        for piece in range(PIECES):
            slots[slot_of(sc, piece), sc[0] ^ fp] = wide[piece * step : (piece + 1) * step, :]
    sums[...] = jnp.sum(g_proj[...].astype(F32), axis=0, keepdims=True)


def first_back_kernel(sc, own, got, far, x, table, g_residual, input_grad, rows_out):
    upstream = own[...] + got[0].astype(F32) + far[...].astype(F32)
    scaled, inverse = normalise(x[...].astype(F32))
    through = norm_back(upstream, scaled, inverse, table[0:1, :])
    input_grad[...] = (g_residual[...] + through).astype(BF16)
    rows_out[0:1, :] = jnp.sum(upstream * scaled, axis=0, keepdims=True)
    rows_out[1:2, :] = jnp.sum(upstream, axis=0, keepdims=True)


def output_kernel(sc, own, got, far, residual, table, out):
    value = (
        residual[...] + own[...] + got[0].astype(F32) + far[...].astype(F32) + table[5:6, :]
    )
    out[...] = jnp.where(valid_rows(sc, sc[0], out.shape[0]), value, 0.0).astype(BF16)


def feed_final_kernel(sc, pieces, proj_out, fc_out):
    step_rows, step_cols = pieces.shape[2], pieces.shape[3]
    quarter = step_rows // WAYS
    for r in range(PIECES):
        piece = (sc[1] ^ reverse(r)) & 7
        a, b = piece >> 1, piece & 1
        cols = block_rows(b, step_cols)
        proj_out[block_rows(a, step_rows), cols] = pieces[r, 0].astype(F32)
        for k in range(WAYS):
            wide = block_rows((sc[0] ^ k) * 2 + b, step_cols)
            fc_out[block_rows(a, quarter), wide] = pieces[
                r, 1, k * quarter : (k + 1) * quarter, :
            ].astype(F32)


def out_final_kernel(sc, pieces, out):
    step_rows, step_cols = pieces.shape[1], pieces.shape[2]
    for r in range(PIECES):
        piece = (sc[1] ^ reverse(r)) & 7
        out[block_rows(piece >> 1, step_rows), block_rows(piece & 1, step_cols)] = pieces[r].astype(F32)


def qkv_final_kernel(sc, pieces, out):
    step, width = pieces.shape[2], pieces.shape[3] // 3
    for r in range(PIECES):
        place = block_rows((sc[1] ^ reverse(r)) & 7, step)
        for fp in range(WAYS):
            piece = pieces[r, sc[0] ^ fp].astype(F32)
            for part in range(3):
                base = part * WAYS * width + fp * width
                out[place, base : base + width] = piece[:, part * width : (part + 1) * width]


def body(
    inputs, lengths, ln1_gain, ln1_bias, qkv_weight, qv_bias, out_weight, out_bias,
    ln2_gain, ln2_bias, fc_weight, fc_bias, proj_weight, proj_bias, cotangent,
):
    group = lax.axis_size("ctx")
    members = group // WAYS
    assert lax.axis_size("fsdp") == WAYS and inputs.shape[0] == 1
    assert group % PIECES == 0 and group & (group - 1) == 0
    f, c = lax.axis_index("fsdp"), lax.axis_index("ctx")
    rows, width = inputs.shape[1:]
    head_width = width // WAYS
    hidden_width = fc_bias.shape[0]
    total = rows * WAYS
    f_order = f ^ jnp.arange(WAYS)

    x_own = swap_layout(inputs[0])
    cot_own = swap_layout(cotangent[0])
    length_digits = jnp.stack([lengths[0] >> 6, lengths[0] & 63]).astype(BF16)
    small = jnp.concatenate(
        [ln1_gain, ln1_bias, out_bias, ln2_gain, ln2_bias, proj_bias, qv_bias, length_digits]
    )
    small_all = jnp.stack([small, f_xor(small, 1), f_xor(small, 2), f_xor(small, 3)])
    small_all = jnp.take(small_all, f_order, axis=0).astype(F32)
    table = jnp.transpose(
        small_all[:, : 6 * head_width].reshape(WAYS, 6, head_width), (1, 0, 2)
    ).reshape(6, width)
    qv_full = small_all[:, 6 * head_width : 8 * head_width].reshape(2 * WAYS, head_width)
    qkv_bias = jnp.concatenate(
        [qv_full[f], jnp.zeros((head_width,), F32), qv_full[WAYS + f]]
    ).reshape(1, 3 * head_width)
    digits = small_all[c // members, 8 * head_width :].astype(jnp.int32)
    sc = jnp.stack(
        [f, c, c % members, jnp.asarray(members), digits[0] * 64 + digits[1]]
    ).astype(jnp.int32)

    qkv_blocks = qkv_weight.reshape(head_width, 3, WAYS, head_width)
    fc_blocks = fc_weight.reshape(head_width, WAYS, hidden_width)

    def columns(blocks, axis, k):
        return lax.dynamic_index_in_dim(blocks, f ^ k, axis, keepdims=False).reshape(
            head_width, -1
        )

    w_qkv = [columns(qkv_blocks, 2, k) for k in range(WAYS)]
    w_fc = [columns(fc_blocks, 1, k) for k in range(WAYS)]
    w_qkv = [w_qkv[0]] + [f_xor(w_qkv[k], k) for k in range(1, WAYS)]
    x_all = gather_f(x_own)
    normed_one, qkv_full, q, kv = call(
        qkv_kernel,
        [
            shape((total, width), BF16),
            shape((width, 3 * head_width), BF16),
            shape((total, head_width), BF16),
            shape((total, 2 * head_width), BF16),
        ],
        [sc, *x_all, *w_qkv, table, qkv_bias],
        flops=2 * total * width * 3 * head_width,
        name="qkv",
    )
    kv_other = [kv] + [c_xor(kv, r) for r in range(1, members)]
    w_fc = [w_fc[0]] + [f_xor(w_fc[k], k) for k in range(1, WAYS)]
    cot_all = gather_f(cot_own)
    g_out, pulled, proj_row = call(
        cot_kernel,
        [shape((total, width), BF16), shape((total, hidden_width), F32), shape((1, width), F32)],
        [sc, *cot_all, proj_weight],
        flops=2 * total * width * hidden_width,
        name="cot",
    )

    partials = [shape((rows, width), F32), shape((rows, width), F32), shape((2, rows, width), BF16)]
    state = []
    for r in range(members):
        first, last = r == 0, r == members - 1
        if last:
            outs = [
                shape((total, head_width), F32),
                shape((total, head_width), BF16),
                shape((total, head_width + 64), BF16),
                *partials,
            ]
            scratch = [pltpu.VMEM((total, width), F32)]
            extra = [out_weight]
        else:
            outs = [shape((total, head_width), F32), shape((total, 128), F32)]
            scratch, extra = [], []

        def kernel(sc_ref, *refs, r=r, first=first, last=last):
            attend(sc_ref, r, first, last, refs)

        state = call(
            kernel,
            outs,
            [sc, q, kv_other[r], *state, *extra],
            scratch,
            flops=4 * total * total * head_width,
            name=f"attend{min(r, 1)}",
        )
    attended, attended_low, q_ext, *branch = state
    q_other = [q_ext] + [c_xor(q_ext, r) for r in range(1, members)]
    branch = scatter_f(*branch)
    residual, normed_two = call(
        second_norm_kernel,
        [shape((rows, width), F32), shape((rows, width), BF16)],
        [sc, *branch, x_own, table],
        name="norm2",
    )
    normed_two_all = gather_f(normed_two)
    normed_two_full, fc_full, active, g_hidden, fc_row, *g_two = call(
        feed_kernel,
        [
            shape((total, width), BF16),
            shape((width, hidden_width), BF16),
            shape((total, hidden_width), BF16),
            shape((total, hidden_width), BF16),
            shape((1, hidden_width), F32),
            *partials,
        ],
        [sc, *normed_two_all, *w_fc, fc_bias.astype(F32).reshape(1, -1), pulled],
        [pltpu.VMEM((total, width), F32)],
        flops=4 * total * width * hidden_width,
        name="feed",
    )
    g_two = scatter_f(*g_two)
    g_residual, g_branch, two_rows = call(
        second_back_kernel,
        [shape((rows, width), F32), shape((rows, width), BF16), shape((3, width), F32)],
        [sc, *g_two, residual, cot_own, table],
        name="norm2_back",
    )
    g_branch_all = gather_f(g_branch)
    g_branch_full, do_ext = call(
        pull_kernel,
        [shape((total, width), BF16), shape((total, head_width + 64), BF16)],
        [sc, *g_branch_all, out_weight, attended],
        flops=2 * total * width * head_width,
        name="pull",
    )
    do_other = [do_ext] + [c_xor(do_ext, r) for r in range(1, members)]
    grads = call(
        back_first,
        [shape((total, head_width), F32), shape((total, 2 * head_width), F32)],
        [sc, q_ext, do_ext, kv],
        flops=10 * total * total * head_width,
        name="back0",
    )
    for r in range(1, members):
        last = r == members - 1
        outs = [shape((total, head_width), F32), shape((total, 2 * head_width), F32)]
        if last:
            scratch = [pltpu.VMEM(o.shape, F32) for o in outs] + [pltpu.VMEM((total, width), F32)]
            outs = [shape((total, 3 * head_width), BF16), *partials]
            extra = [qkv_full]
        else:
            scratch, extra = [], []

        def kernel(sc_ref, *refs, r=r, last=last):
            back_step(sc_ref, r, last, refs)

        grads = call(
            kernel,
            outs,
            [sc, q_ext, do_ext, kv, q_other[r], do_other[r], kv_other[r], *grads, *extra],
            scratch,
            flops=14 * total * total * head_width,
            name="back1",
        )
    g_proj, *g_one = grads
    g_one = scatter_f(*g_one)
    step = head_width // PIECES
    qkv_slots, qkv_sums = call(
        qkv_grad_kernel,
        [shape((PIECES, WAYS, step, 3 * head_width), BF16), shape((1, 3 * head_width), F32)],
        [sc, normed_one, g_proj],
        flops=2 * total * width * 3 * head_width,
        name="qkv_grad",
    )
    input_grad, one_rows = call(
        first_back_kernel,
        [shape((rows, width), BF16), shape((2, width), F32)],
        [sc, *g_one, x_own, table, g_residual],
        name="norm1_back",
    )
    input_grad = swap_layout(input_grad)[None]

    result = call(
        result_kernel,
        partials,
        [sc, active, proj_weight],
        [pltpu.VMEM((total, width), F32)],
        flops=2 * total * width * hidden_width,
        name="result",
    )
    result = scatter_f(*result)
    (outputs,) = call(
        output_kernel, [shape((rows, width), BF16)], [sc, *result, residual, table], name="output"
    )
    outputs = swap_layout(outputs)[None]

    (feed_slots,) = call(
        feed_grad_kernel,
        [shape((PIECES, 2, head_width, width // 2), BF16)],
        [sc, active, g_out, normed_two_full, g_hidden],
        flops=4 * total * width * hidden_width,
        name="feed_grad",
    )
    quarter = head_width // WAYS
    feed_piece = reduce_c(feed_slots)
    fc_piece = feed_piece[1].reshape(WAYS, quarter, width // 2)
    fc_piece = jnp.stack([fc_piece[0]] + [f_xor(fc_piece[k], k) for k in range(1, WAYS)])
    feed_piece = jnp.stack([feed_piece[0], fc_piece.reshape(head_width, width // 2)])
    grad_proj, grad_fc = call(
        feed_final_kernel,
        [shape((hidden_width, width), F32), shape((head_width, WAYS * hidden_width), F32)],
        [sc, gather_c(feed_piece)],
        name="feed_final",
    )
    (out_slots,) = call(
        out_grad_kernel,
        [shape((PIECES, quarter, width // 2), BF16)],
        [sc, attended_low, g_branch_full],
        flops=2 * total * width * head_width,
        name="out_grad",
    )
    (grad_out,) = call(
        out_final_kernel,
        [shape((head_width, width), F32)],
        [sc, gather_c(reduce_c(out_slots))],
        name="out_final",
    )
    qkv_piece = reduce_c(qkv_slots)
    qkv_piece = jnp.stack([qkv_piece[0]] + [f_xor(qkv_piece[k], k) for k in range(1, WAYS)])
    (grad_qkv,) = call(
        qkv_final_kernel,
        [shape((head_width, 3 * width), F32)],
        [sc, gather_c(qkv_piece)],
        name="qkv_final",
    )

    here = (jnp.arange(WAYS) == f)[:, None]
    q_row = jnp.where(here, qkv_sums[:, :head_width], 0.0).reshape(1, width)
    v_row = jnp.where(here, qkv_sums[:, 2 * head_width :], 0.0).reshape(1, width)
    fc_rows = jnp.where(here, fc_row, 0.0)
    early = sum_all(jnp.concatenate([two_rows, proj_row, fc_rows], axis=0))
    late = sum_all(jnp.concatenate([one_rows, q_row, v_row], axis=0))

    def mine(row):
        return lax.dynamic_slice_in_dim(row, f * head_width, head_width, 0)

    grad_qv = lax.dynamic_slice_in_dim(
        jnp.concatenate([late[2], late[3]]), f * 2 * head_width, 2 * head_width, 0
    )
    grad_fc_bias = lax.dynamic_index_in_dim(early[4:], f, 0, keepdims=False)
    return (
        outputs,
        input_grad,
        mine(late[0]),
        mine(late[1]),
        grad_qkv,
        grad_qv,
        grad_out,
        mine(early[2]),
        mine(early[0]),
        mine(early[1]),
        grad_fc,
        grad_fc_bias,
        grad_proj,
        mine(early[3]),
    )


def solution(mesh):
    tokens, rows, vector = P("fsdp", "ctx", None), P("fsdp", None), P("fsdp")
    in_specs = (
        tokens, vector, vector, vector, rows, vector, rows, vector,
        vector, vector, rows, vector, rows, vector, tokens,
    )
    out_specs = (
        tokens, tokens, vector, vector, rows, vector, rows, vector,
        vector, vector, rows, vector, rows, vector,
    )
    return jax.shard_map(body, mesh=mesh, in_specs=in_specs, out_specs=out_specs, check_vma=False)
```

time: 883 us -> 324 us (0.37)
  the two profiles are of different devices: /device:TPU:0 before, /device:TPU:6 now
where the time goes in v1:
time: 324 us; the launch traced here: 318 us
  waiting for transfers between devices  140 us (43%)
  starting transfers between devices  69 us (21%)
  Pallas kernels  57.4 us (18%)
  local copies, waits for them, and re-layouts  39 us (12%)
  other arithmetic  8.04 us (2%)
  between operations  3.91 us (1%)
    ppermute x27, waiting for transfers between devices, c_xor(): return lax.ppermute(x, 'ctx', [(i, i ^ k) for i in range(n)])  78 us
    pallas_call x19, Pallas kernels, call(): pl.pallas_call(kernel, out_shape=tuple(outs), in_specs=[pl.BlockSpec(memo...  57.4 us
    ppermute x39, waiting for transfers between devices, f_xor(): return lax.ppermute(x, 'fsdp', [(i, i ^ k) for i in range(n)])  43.9 us
    ppermute x27, starting transfers between devices, c_xor(): return lax.ppermute(x, 'ctx', [(i, i ^ k) for i in range(n)])  31.3 us
    ppermute x39, starting transfers between devices, f_xor(): return lax.ppermute(x, 'fsdp', [(i, i ^ k) for i in range(n)])  21.2 us
    ppermute x4, waiting for transfers between devices, swap_layout(): return lax.ppermute(x, ('fsdp', 'ctx'), perm)  18.5 us
    ppermute x4, starting transfers between devices, swap_layout(): return lax.ppermute(x, ('fsdp', 'ctx'), perm)  16.5 us
    unnamed x70, local copies, waits for them, and re-layouts  14 us
  transfers between devices with their start and end apart: 70, of which 28 were waited for; matrix products, arithmetic and copies ran while one was open for 10% of the time, Pallas kernels for 13%

profile of v1, /device:TPU:6, one launch (start us, length us, event | category | flops | bytes accessed | tf_op | source)
XLA Modules:
  0.0 317.7 jit_solution(3487695996283052177)
XLA Ops:
  1.3 4.8 %concatenate.49 = bf16[1538]{0:T(1024)(128)(2,1)S(1)} concatenate(bf16[192]{0:T(256)(128)(2,1)} %param.17, bf16[192]{0:T(256)(128)(2,1)} %param.18, bf16[192]{0:T(256)(128)(2,1)} %param.22, bf16[192]{0:T(256)(128)(2,1)} %param.23, bf16[192]{0:T(256)(128)(2,1)} %param.24, bf16[192]{0:T(256)(128)(2,1)} %param.28, bf16[384]{0:T(512)(128)(2,1)} %param.20, bf16[1]{0:T(256)(128)(2,1)S(6)} %convert.11, ...), dimensions={0} | concatenate | bytes 6152 | tf_op jit(solution)/shard_map/concatenate | solution.py:527
  7.9 4.4 %collective-permute-start.3 = (bf16[128,768]{1,0:T(8,128)(2,1)}, bf16[128,768]{1,0:T(8,128)(2,1)S(1)}, u32[]{:S(2)}, u32[]{:S(2)}) collective-permute-start(bf16[128,768]{1,0:T(8,128)(2,1)} %bitcast.113), channel_id=1, source_target_pairs={{0,0},{1,1},{2,8},{3,9},{4,16},{5,17},{6,24},{7,25},{8,2},{9,3},{1... | collective-permute-start | bytes 589832 | tf_op jit(solution)/shard_map/ppermute | solution.py:37
  28.8 14.0 %collective-permute-done.5.x2 = bf16[128,768]{1,0:T(8,128)(2,1)S(1)} collective-permute-done((bf16[128,768]{1,0:T(8,128)(2,1)S(1)}, bf16[128,768]{1,0:T(8,128)(2,1)S(1)}, u32[]{:S(2)}, u32[]{:S(2)}) %collective-permute-start.5) | collective-permute-done | bytes 196640 | tf_op jit(solution)/shard_map/ppermute | solution.py:21
  48.1 4.0 %attend0.1 = (f32[512,192]{1,0:T(8,128)S(1)}, f32[512,128]{1,0:T(8,128)S(1)}) custom-call(s32[5]{0:T(128)S(1)} %stack.70.sc.sc_ref, bf16[512,192]{1,0:T(8,128)(2,1)S(1)} %get-tuple-element.58.refs_0_, bf16[512,384]{1,0:T(8,128)(2,1)S(1)} %get-tuple-element.59.refs_1_.kv.refs_2_), custom_call_target="tpu_custom_call" | custom-call | flops 201326592 | bytes 1245204 | tf_op jit(solution)/shard_map/attend0/pallas_call | solution.py:89
  52.2 6.9 %collective-permute-done.10.refs_1_.refs_5_ = bf16[512,384]{1,0:T(8,128)(2,1)S(1)} collective-permute-done((bf16[512,384]{1,0:T(8,128)(2,1)S(1)}, bf16[512,384]{1,0:T(8,128)(2,1)S(1)}, u32[]{:S(2)}, u32[]{:S(2)}) %collective-permute-start.10) | collective-permute-done | bytes 393248 | tf_op jit(solution)/shard_map/ppermute | solution.py:26
  59.1 6.5 %attend1.1 = (f32[512,192]{1,0:T(8,128)S(1)}, bf16[512,192]{1,0:T(8,128)(2,1)S(1)}, bf16[512,256]{1,0:T(8,128)(2,1)S(1)}, f32[128,768]{1,0:T(8,128)S(1)}, f32[12...) custom-call(s32[5]{0:T(128)S(1)} %stack.70.sc.sc_ref, bf16[512,192]{1,0:T(8,128)(2,1)S(1)} %get-tuple-element.58.refs_0_, ...), custom_call_target="tpu_custom_call" | custom-call | flops 201326592 | bytes 3571732 | tf_op jit(solution)/shard_map/attend1/pallas_call | solution.py:89
  69.0 11.5 %collective-permute-done.19.c0.cot = bf16[128,768]{1,0:T(8,128)(2,1)S(1)} collective-permute-done((bf16[128,768]{1,0:T(8,128)(2,1)S(1)}, bf16[128,768]{1,0:T(8,128)(2,1)S(1)}, u32[]{:S(2)}, u32[]{:S(2)}) %collective-permute-start.19) | collective-permute-done | bytes 196640 | tf_op jit(solution)/shard_map/ppermute | solution.py:37
  82.7 3.8 %reshape.197 = bf16[192,4,768]{2,1,0:T(4,128)(2,1)} reshape(bf16[192,3072]{1,0:T(8,128)(2,1)} %param.25) | data formatting | bytes 2359296 | tf_op jit(solution)/shard_map/reshape | solution.py:545
  102.4 5.8 %collective-permute-done.18.w3 = bf16[192,768]{1,0:T(8,128)(2,1)S(1)} collective-permute-done((bf16[192,768]{1,0:T(8,128)(2,1)S(1)}, bf16[192,768]{1,0:T(8,128)(2,1)S(1)}, u32[]{:S(2)}, u32[]{:S(2)}) %collective-permute-start.18) | collective-permute-done | bytes 294944 | tf_op jit(solution)/shard_map/ppermute | solution.py:21
  108.3 4.9 %feed.1 = (bf16[512,768]{1,0:T(8,128)(2,1)S(1)}, bf16[768,768]{1,0:T(8,128)(2,1)}, bf16[512,768]{1,0:T(8,128)(2,1)S(1)}, bf16[512,768]{1,0:T(8,128)(2,1)S(1)}, f...) custom-call(s32[5]{0:T(128)S(1)} %stack.70.sc.sc_ref, ...), custom_call_target="tpu_custom_call" | custom-call | flops 1207959552 | bytes 8263700 | tf_op jit(solution)/shard_map/feed/pallas_call | solution.py:89
  123.9 5.1 %collective-permute-done.27.far = bf16[128,768]{1,0:T(8,128)(2,1)S(1)} collective-permute-done((bf16[128,768]{1,0:T(8,128)(2,1)S(1)}, bf16[128,768]{1,0:T(8,128)(2,1)S(1)}, u32[]{:S(2)}, u32[]{:S(2)}) %collective-permute-start.27) | collective-permute-done | bytes 196640 | tf_op jit(solution)/shard_map/ppermute | solution.py:21
  138.7 8.4 %collective-permute-done.57 = f32[8,768]{1,0:T(8,128)S(1)} collective-permute-done((f32[8,768]{1,0:T(8,128)S(1)}, f32[8,768]{1,0:T(8,128)S(1)}, u32[]{:S(2)}, u32[]{:S(2)}) %collective-permute-start.57) | collective-permute-done | bytes 24608 | tf_op jit(solution)/shard_map/ppermute | solution.py:21
  161.9 3.5 %collective-permute-start.25 = (bf16[128,768]{1,0:T(8,128)(2,1)}, bf16[128,768]{1,0:T(8,128)(2,1)}, u32[]{:S(2)}, u32[]{:S(2)}) collective-permute-start(bf16[128,768]{1,0:T(8,128)(2,1)} %output.1), channel_id=1, source_target_pairs={{0,0},{1,1},{2,8},{3,9},{4,16},{5,17},{6,24},{7,25},{8,2},{9,3},{1... | collective-permute-start | bytes 589832 | tf_op jit(solution)/shard_map/ppermute | solution.py:37
  173.7 6.3 %back0.1 = (f32[512,192]{1,0:T(8,128)S(1)}, f32[512,384]{1,0:T(8,128)S(1)}) custom-call(s32[5]{0:T(128)S(1)} %stack.70.sc.sc_ref, bf16[512,256]{1,0:T(8,128)(2,1)S(1)} %copy-done.18, bf16[512,256]{1,0:T(8,128)(2,1)S(1)} %get-tuple-element.78.do.refs_1_, bf16[512,384]{1,0:T(8,128)(2,1)S(1)} %copy-done.7), custom_call_target="tpu_custom_call" | custom-call | flops 503316480 | bytes 2097172 | tf_op jit(solution)/shard_map/back0/pallas_call | solution.py:89
  184.7 10.1 %back1.1 = (bf16[512,576]{1,0:T(8,128)(2,1)S(1)}, f32[128,768]{1,0:T(8,128)S(1)}, f32[128,768]{1,0:T(8,128)S(1)}, bf16[2,128,768]{2,1,0:T(8,128)(2,1)S(1)}) custom-call(s32[5]{0:T(128)S(1)} %stack.70.sc.sc_ref, bf16[512,256]{1,0:T(8,128)(2,1)S(1)} %copy-done.18, bf16[512,256]{1,0:T(8,128)(2,1)S(1)} %get-tuple-element.78.do.refs_1_, ...), custom_call_target="tpu_custom_call" | custom-call | flops 704643072 | bytes 5668884 | tf_op jit(solution)/shard_map/back1/pallas_call | solution.py:89
  205.5 11.0 %collective-permute-done.63 = bf16[1,2,192,384]{3,2,1,0:T(8,128)(2,1)} collective-permute-done((bf16[1,2,192,384]{3,2,1,0:T(8,128)(2,1)}, bf16[1,2,192,384]{3,2,1,0:T(8,128)(2,1)}, u32[]{:S(2)}, u32[]{:S(2)}) %collective-permute-start.63) | collective-permute-done | bytes 294944 | tf_op jit(solution)/shard_map/ppermute | solution.py:26
  226.0 12.6 %collective-permute-done.67 = bf16[1,2,192,384]{3,2,1,0:T(8,128)(2,1)S(1)} collective-permute-done((bf16[1,2,192,384]{3,2,1,0:T(8,128)(2,1)S(1)}, bf16[1,2,192,384]{3,2,1,0:T(8,128)(2,1)S(1)}, u32[]{:S(2)}, u32[]{:S(2)}) %collective-permute-start.67) | collective-permute-done | bytes 294944 | tf_op jit(solution)/shard_map/ppermute | solution.py:26
  241.5 13.4 %collective-permute-done.43 = bf16[1,4,24,576]{3,2,1,0:T(8,128)(2,1)S(1)} collective-permute-done((bf16[1,4,24,576]{3,2,1,0:T(8,128)(2,1)S(1)}, bf16[1,4,24,576]{3,2,1,0:T(8,128)(2,1)S(1)}, u32[]{:S(2)}, u32[]{:S(2)}) %collective-permute-start.43) | collective-permute-done | bytes 110624 | tf_op jit(solution)/shard_map/ppermute | solution.py:26
  260.4 3.4 %collective-permute-start.47 = (bf16[1,4,24,576]{3,2,1,0:T(8,128)(2,1)S(1)}, bf16[1,4,24,576]{3,2,1,0:T(8,128)(2,1)S(1)}, u32[]{:S(2)}, u32[]{:S(2)}) collective-permute-start(bf16[1,4,24,576]{3,2,1,0:T(8,128)(2,1)S(1)} %maximum_bitcast_fusion.1), channel_id=1, source_target_pairs={{0,4},{1,5},{2,6},{3,7},{4,0},{5,1},{6,2},{7,3},{8,12},{9,13},{10,... | collective-permute-start | bytes 331784 | tf_op jit(solution)/shard_map/ppermute | solution.py:26
  265.1 4.4 %collective-permute-done.47 = bf16[1,4,24,576]{3,2,1,0:T(8,128)(2,1)S(1)} collective-permute-done((bf16[1,4,24,576]{3,2,1,0:T(8,128)(2,1)S(1)}, bf16[1,4,24,576]{3,2,1,0:T(8,128)(2,1)S(1)}, u32[]{:S(2)}, u32[]{:S(2)}) %collective-permute-start.47) | collective-permute-done | bytes 110624 | tf_op jit(solution)/shard_map/ppermute | solution.py:26
  273.1 16.5 %collective-permute-done.55 = bf16[4,48,384]{2,1,0:T(8,128)(2,1)S(1)} collective-permute-done((bf16[4,48,384]{2,1,0:T(8,128)(2,1)S(1)}, bf16[4,48,384]{2,1,0:T(8,128)(2,1)S(1)}, u32[]{:S(2)}, u32[]{:S(2)}) %collective-permute-start.55) | collective-permute-done | bytes 147488 | tf_op jit(solution)/shard_map/ppermute | solution.py:26
  291.1 6.0 %collective-permute-start.35 = (bf16[128,768]{1,0:T(8,128)(2,1)S(1)}, bf16[128,768]{1,0:T(8,128)(2,1)S(1)}, u32[]{:S(2)}, u32[]{:S(2)}) collective-permute-start(bf16[128,768]{1,0:T(8,128)(2,1)S(1)} %get-tuple-element.86), channel_id=1, source_target_pairs={{0,0},{1,1},{2,8},{3,9},{4,16},{5,17},{6,24},{7,25},{8,2},{9,3},{1... | collective-permute-start | bytes 589832 | tf_op jit(solution)/shard_map/ppermute | solution.py:37
  299.2 6.9 %collective-permute-done.35 = bf16[128,768]{1,0:T(8,128)(2,1)S(1)} collective-permute-done((bf16[128,768]{1,0:T(8,128)(2,1)S(1)}, bf16[128,768]{1,0:T(8,128)(2,1)S(1)}, u32[]{:S(2)}, u32[]{:S(2)}) %collective-permute-start.35) | collective-permute-done | bytes 196640 | tf_op jit(solution)/shard_map/ppermute | solution.py:37
  306.1 3.6 %collective-permute-done.49 = bf16[4,4,24,576]{3,2,1,0:T(8,128)(2,1)S(1)} collective-permute-done((bf16[4,4,24,576]{3,2,1,0:T(8,128)(2,1)S(1)}, bf16[4,4,24,576]{3,2,1,0:T(8,128)(2,1)S(1)}, u32[]{:S(2)}, u32[]{:S(2)}) %collective-permute-start.49) | collective-permute-done | bytes 442400 | tf_op jit(solution)/shard_map/ppermute | solution.py:26
  (302 shorter events, 135.8 us)
Async XLA Ops:
  6.1 19.3 %collective-permute-start.2 = (bf16[1538]{0:T(1024)(128)(2,1)S(1)}, bf16[1538]{0:T(1024)(128)(2,1)S(1)}, u32[]{:S(2)}, u32[]{:S(2)}) collective-permute-start(bf16[1538]{0:T(1024)(128)(2,1)S(1)} %concatenate.49), channel_id=1, source_target_pairs={{0,24},{8,16},{16,8},{24,0},{1,25},{9,17},{17,9},{25,1},{2,26},{10... | collective-permute-start | bytes 9236 | tf_op jit(solution)/shard_map/ppermute | solution.py:21
  6.1 19.4 %collective-permute-start.1 = (bf16[1538]{0:T(1024)(128)(2,1)S(1)}, bf16[1538]{0:T(1024)(128)(2,1)S(1)}, u32[]{:S(2)}, u32[]{:S(2)}) collective-permute-start(bf16[1538]{0:T(1024)(128)(2,1)S(1)} %concatenate.49), channel_id=1, source_target_pairs={{0,16},{8,24},{16,0},{24,8},{1,17},{9,25},{17,1},{25,9},{2,18},{10... | collective-permute-start | bytes 9236 | tf_op jit(solution)/shard_map/ppermute | solution.py:21
  7.5 19.3 %collective-permute-start = (bf16[1538]{0:T(1024)(128)(2,1)S(1)}, bf16[1538]{0:T(1024)(128)(2,1)S(1)}, u32[]{:S(2)}, u32[]{:S(2)}) collective-permute-start(bf16[1538]{0:T(1024)(128)(2,1)S(1)} %concatenate.49), channel_id=1, source_target_pairs={{0,8},{8,0},{16,24},{24,16},{1,9},{9,1},{17,25},{25,17},{2,10},{10... | collective-permute-start | bytes 9236 | tf_op jit(solution)/shard_map/ppermute | solution.py:21
  7.9 19.9 %collective-permute-start.3 = (bf16[128,768]{1,0:T(8,128)(2,1)}, bf16[128,768]{1,0:T(8,128)(2,1)S(1)}, u32[]{:S(2)}, u32[]{:S(2)}) collective-permute-start(bf16[128,768]{1,0:T(8,128)(2,1)} %bitcast.113), channel_id=1, source_target_pairs={{0,0},{1,1},{2,8},{3,9},{4,16},{5,17},{6,24},{7,25},{8,2},{9,3},{1... | collective-permute-start | bytes 589832 | tf_op jit(solution)/shard_map/ppermute | solution.py:37
  20.8 24.0 %collective-permute-start.7 = (bf16[192,576]{1,0:T(8,128)(2,1)}, bf16[192,576]{1,0:T(8,128)(2,1)S(1)}, u32[]{:S(2)}, u32[]{:S(2)}) collective-permute-start(bf16[192,576]{1,0:T(8,128)(2,1)} %copy.40), channel_id=1, source_target_pairs={{0,8},{8,0},{16,24},{24,16},{1,9},{9,1},{17,25},{25,17},{2,10},{10... | collective-permute-start | bytes 663560 | tf_op jit(solution)/shard_map/ppermute | solution.py:21
  25.4 19.4 %collective-permute-start.8 = (bf16[192,576]{1,0:T(8,128)(2,1)S(1)}, bf16[192,576]{1,0:T(8,128)(2,1)S(1)}, u32[]{:S(2)}, u32[]{:S(2)}) collective-permute-start(bf16[192,576]{1,0:T(8,128)(2,1)S(1)} %copy.42), channel_id=1, source_target_pairs={{0,16},{8,24},{16,0},{24,8},{1,17},{9,25},{17,1},{25,9},{2,18},{10... | collective-permute-start | bytes 663560 | tf_op jit(solution)/shard_map/ppermute | solution.py:21
  25.5 19.3 %collective-permute-start.9 = (bf16[192,576]{1,0:T(8,128)(2,1)S(1)}, bf16[192,576]{1,0:T(8,128)(2,1)S(1)}, u32[]{:S(2)}, u32[]{:S(2)}) collective-permute-start(bf16[192,576]{1,0:T(8,128)(2,1)S(1)} %copy.44), channel_id=1, source_target_pairs={{0,24},{8,16},{16,8},{24,0},{1,25},{9,17},{17,9},{25,1},{2,26},{10... | collective-permute-start | bytes 663560 | tf_op jit(solution)/shard_map/ppermute | solution.py:21
  120.6 60.2 %collective-permute-start.61 = (bf16[4,2,192,384]{3,2,1,0:T(8,128)(2,1)}, bf16[4,2,192,384]{3,2,1,0:T(8,128)(2,1)}, u32[]{:S(2)}, u32[]{:S(2)}) collective-permute-start(bf16[4,2,192,384]{3,2,1,0:T(8,128)(2,1)} %slice.240), channel_id=1, source_target_pairs={{0,1},{1,0},{2,3},{3,2},{4,5},{5,4},{6,7},{7,6},{8,9},{9,8},{10,11... | collective-permute-start | bytes 3538952 | tf_op jit(solution)/shard_map/ppermute | solution.py:26
  134.8 24.2 %collective-permute-start.24 = (bf16[128,768]{1,0:T(8,128)(2,1)}, bf16[128,768]{1,0:T(8,128)(2,1)}, u32[]{:S(2)}, u32[]{:S(2)}) collective-permute-start(bf16[128,768]{1,0:T(8,128)(2,1)} %fusion.2), channel_id=1, source_target_pairs={{0,16},{8,24},{16,0},{24,8},{1,17},{9,25},{17,1},{25,9},{2,18},{10... | collective-permute-start | bytes 589832 | tf_op jit(solution)/shard_map/ppermute | solution.py:21
  136.5 28.8 %collective-permute-start.29 = (bf16[128,768]{1,0:T(8,128)(2,1)}, bf16[128,768]{1,0:T(8,128)(2,1)}, u32[]{:S(2)}, u32[]{:S(2)}) collective-permute-start(bf16[128,768]{1,0:T(8,128)(2,1)} %get-tuple-element.76.b0), channel_id=1, source_target_pairs={{0,16},{8,24},{16,0},{24,8},{1,17},{9,25},{17,1},{25,9},{2,18},{10... | collective-permute-start | bytes 589832 | tf_op jit(solution)/shard_map/ppermute | solution.py:21
  157.5 27.1 %collective-permute-start.31 = (bf16[512,256]{1,0:T(8,128)(2,1)}, bf16[512,256]{1,0:T(8,128)(2,1)S(1)}, u32[]{:S(2)}, u32[]{:S(2)}) collective-permute-start(bf16[512,256]{1,0:T(8,128)(2,1)} %copy-done.17), channel_id=1, source_target_pairs={{0,1},{1,0},{2,3},{3,2},{4,5},{5,4},{6,7},{7,6},{8,9},{9,8},{10,11... | collective-permute-start | bytes 786440 | tf_op jit(solution)/shard_map/ppermute | solution.py:26
  161.9 108.9 %collective-permute-start.25 = (bf16[128,768]{1,0:T(8,128)(2,1)}, bf16[128,768]{1,0:T(8,128)(2,1)}, u32[]{:S(2)}, u32[]{:S(2)}) collective-permute-start(bf16[128,768]{1,0:T(8,128)(2,1)} %output.1), channel_id=1, source_target_pairs={{0,0},{1,1},{2,8},{3,9},{4,16},{5,17},{6,24},{7,25},{8,2},{9,3},{1... | collective-permute-start | bytes 589832 | tf_op jit(solution)/shard_map/ppermute | solution.py:37
  182.5 16.7 %collective-permute-start.62 = (bf16[2,2,192,384]{3,2,1,0:T(8,128)(2,1)S(1)}, bf16[2,2,192,384]{3,2,1,0:T(8,128)(2,1)S(1)}, u32[]{:S(2)}, u32[]{:S(2)}) collective-permute-start(bf16[2,2,192,384]{3,2,1,0:T(8,128)(2,1)S(1)} %slice.242), channel_id=1, source_target_pairs={{0,2},{1,3},{2,0},{3,1},{4,6},{5,7},{6,4},{7,5},{8,10},{9,11},{10,... | collective-permute-start | bytes 1769480 | tf_op jit(solution)/shard_map/ppermute | solution.py:26
  200.1 16.4 %collective-permute-start.63 = (bf16[1,2,192,384]{3,2,1,0:T(8,128)(2,1)}, bf16[1,2,192,384]{3,2,1,0:T(8,128)(2,1)}, u32[]{:S(2)}, u32[]{:S(2)}) collective-permute-start(bf16[1,2,192,384]{3,2,1,0:T(8,128)(2,1)} %slice.244), channel_id=1, source_target_pairs={{0,4},{1,5},{2,6},{3,7},{4,0},{5,1},{6,2},{7,3},{8,12},{9,13},{10,... | collective-permute-start | bytes 884744 | tf_op jit(solution)/shard_map/ppermute | solution.py:26
  203.8 20.4 %collective-permute-start.41 = (bf16[4,4,24,576]{3,2,1,0:T(8,128)(2,1)S(1)}, bf16[4,4,24,576]{3,2,1,0:T(8,128)(2,1)S(1)}, u32[]{:S(2)}, u32[]{:S(2)}) collective-permute-start(bf16[4,4,24,576]{3,2,1,0:T(8,128)(2,1)S(1)} %slice.174), channel_id=1, source_target_pairs={{0,1},{1,0},{2,3},{3,2},{4,5},{5,4},{6,7},{7,6},{8,9},{9,8},{10,11... | collective-permute-start | bytes 1327112 | tf_op jit(solution)/shard_map/ppermute | solution.py:26
  221.1 20.3 %collective-permute-start.53 = (bf16[1,48,384]{2,1,0:T(8,128)(2,1)S(1)}, bf16[1,48,384]{2,1,0:T(8,128)(2,1)S(1)}, u32[]{:S(2)}, u32[]{:S(2)}) collective-permute-start(bf16[1,48,384]{2,1,0:T(8,128)(2,1)S(1)} %add_convert_fusion.8), channel_id=1, source_target_pairs={{0,4},{1,5},{2,6},{3,7},{4,0},{5,1},{6,2},{7,3},{8,12},{9,13},{10,... | collective-permute-start | bytes 110600 | tf_op jit(solution)/shard_map/ppermute | solution.py:26
  221.9 16.7 %collective-permute-start.67 = (bf16[1,2,192,384]{3,2,1,0:T(8,128)(2,1)S(1)}, bf16[1,2,192,384]{3,2,1,0:T(8,128)(2,1)S(1)}, u32[]{:S(2)}, u32[]{:S(2)}) collective-permute-start(bf16[1,2,192,384]{3,2,1,0:T(8,128)(2,1)S(1)} %maximum_bitcast_fusion), channel_id=1, source_target_pairs={{0,4},{1,5},{2,6},{3,7},{4,0},{5,1},{6,2},{7,3},{8,12},{9,13},{10,... | collective-permute-start | bytes 884744 | tf_op jit(solution)/shard_map/ppermute | solution.py:26
  224.7 16.8 %collective-permute-start.37 = (f32[4,768]{1,0:T(4,128)S(1)}, f32[4,768]{1,0:T(4,128)S(1)}, u32[]{:S(2)}, u32[]{:S(2)}) collective-permute-start(f32[4,768]{1,0:T(4,128)S(1)} %fusion.7), channel_id=1, source_target_pairs={{0,16},{8,24},{16,0},{24,8},{1,17},{9,25},{17,1},{25,9},{2,18},{10... | collective-permute-start | bytes 36872 | tf_op jit(solution)/shard_map/ppermute | solution.py:21
  238.7 18.4 %collective-permute-start.68 = (bf16[2,2,192,384]{3,2,1,0:T(8,128)(2,1)S(1)}, bf16[2,2,192,384]{3,2,1,0:T(8,128)(2,1)S(1)}, u32[]{:S(2)}, u32[]{:S(2)}) collective-permute-start(bf16[2,2,192,384]{3,2,1,0:T(8,128)(2,1)S(1)} %pad_maximum_fusion.3), channel_id=1, source_target_pairs={{0,2},{1,3},{2,0},{3,1},{4,6},{5,7},{6,4},{7,5},{8,10},{9,11},{10,... | collective-permute-start | bytes 1769480 | tf_op jit(solution)/shard_map/ppermute | solution.py:26
  241.4 22.5 %collective-permute-start.54 = (bf16[2,48,384]{2,1,0:T(8,128)(2,1)S(1)}, bf16[2,48,384]{2,1,0:T(8,128)(2,1)S(1)}, u32[]{:S(2)}, u32[]{:S(2)}) collective-permute-start(bf16[2,48,384]{2,1,0:T(8,128)(2,1)S(1)} %pad_maximum_fusion.9), channel_id=1, source_target_pairs={{0,2},{1,3},{2,0},{3,1},{4,6},{5,7},{6,4},{7,5},{8,10},{9,11},{10,... | collective-permute-start | bytes 221192 | tf_op jit(solution)/shard_map/ppermute | solution.py:26
  259.0 52.9 %collective-permute-start.69 = (bf16[4,2,192,384]{3,2,1,0:T(8,128)(2,1)S(1)}, bf16[4,2,192,384]{3,2,1,0:T(8,128)(2,1)S(1)}, u32[]{:S(2)}, u32[]{:S(2)}) collective-permute-start(bf16[4,2,192,384]{3,2,1,0:T(8,128)(2,1)S(1)} %pad_maximum_fusion.1), channel_id=1, source_target_pairs={{0,1},{1,0},{2,3},{3,2},{4,5},{5,4},{6,7},{7,6},{8,9},{9,8},{10,11... | collective-permute-start | bytes 3538952 | tf_op jit(solution)/shard_map/ppermute | solution.py:26
  263.9 25.8 %collective-permute-start.55 = (bf16[4,48,384]{2,1,0:T(8,128)(2,1)S(1)}, bf16[4,48,384]{2,1,0:T(8,128)(2,1)S(1)}, u32[]{:S(2)}, u32[]{:S(2)}) collective-permute-start(bf16[4,48,384]{2,1,0:T(8,128)(2,1)S(1)} %pad_maximum_fusion.7), channel_id=1, source_target_pairs={{0,1},{1,0},{2,3},{3,2},{4,5},{5,4},{6,7},{7,6},{8,9},{9,8},{10,11... | collective-permute-start | bytes 442376 | tf_op jit(solution)/shard_map/ppermute | solution.py:26
  269.5 27.6 %collective-permute-start.48 = (bf16[2,4,24,576]{3,2,1,0:T(8,128)(2,1)S(1)}, bf16[2,4,24,576]{3,2,1,0:T(8,128)(2,1)S(1)}, u32[]{:S(2)}, u32[]{:S(2)}) collective-permute-start(bf16[2,4,24,576]{3,2,1,0:T(8,128)(2,1)S(1)} %pad_maximum_fusion.6), channel_id=1, source_target_pairs={{0,2},{1,3},{2,0},{3,1},{4,6},{5,7},{6,4},{7,5},{8,10},{9,11},{10,... | collective-permute-start | bytes 663560 | tf_op jit(solution)/shard_map/ppermute | solution.py:26
  270.8 26.3 %collective-permute-start.40 = (f32[4,768]{1,0:T(4,128)S(1)}, f32[4,768]{1,0:T(4,128)S(1)}, u32[]{:S(2)}, u32[]{:S(2)}) collective-permute-start(f32[4,768]{1,0:T(4,128)S(1)} %add.154), channel_id=1, source_target_pairs={{0,4},{1,5},{2,6},{3,7},{4,0},{5,1},{6,2},{7,3},{8,12},{9,13},{10,... | collective-permute-start | bytes 36872 | tf_op jit(solution)/shard_map/ppermute | solution.py:26
  (76 other events, 588.8 us)
